TPU v7x, 256 devices: a whole 4x4x8 slice. The times are simulated.
256 devices in a mesh: frames: 64 (over y, z, core), tiles: 4 (over x).
Axes of the slice: x: 4, y: 4, z: 8, core: 2. Of those that a mesh axis runs over, the one named last changes fastest.
Arguments:
- frames: bfloat16 [256, 3, 128, 1024], P(('frames', 'tiles')), may hold values from -6 to 6
- weight_map: bfloat16 [256, 128, 1024], P(('frames', 'tiles')), may hold values from 0.049804688 to 1
- seam_mask: int32 [256, 128, 64], P(('frames', 'tiles')), may hold values 0 or 1
- strip_cell: int32 [256], P(('frames', 'tiles')), may hold values from 0 to 60
- partner: int32 [256], P(('frames', 'tiles')), may hold values from 0 to 255, as said below
- tile_group: int32 [256, 32, 1], P(('frames', 'tiles')), may hold values from 0 to 63; in each aligned block of 32 rows (0 to 31, 32 to 63, ..., all dimensions but the last counted through in order) at most 2 rows name the same one
- tile_position_in_group: int32 [256, 32], P(('frames', 'tiles')), may hold values from 0 to 15
Outputs:
- panorama: float32 [1024, 3, 4096], P(('frames', 'tiles'))
Inputs may be any that keep to these rules, and one draw needn't show every extreme that they name: partner[partner[f]] = f. Writing f = (g * 4 + t) + j with t < 4 and j < 1, partner[f] = ((g XOR m_(t,j)) * 4 + t) + j, with one nonzero m_(t,j) below 64 for each pair t, j; among these masks are 32 and 1. `tile_group`: within the rows of one device (32 rows), no value occurs more than 2 times, and some value occurs exactly 2 times.
All inputs are finite; a program needn't handle non-finite values. No bound on the sum of `seam_mask` on one device may be relied on, other than what follows from the above.
Results may differ from a plain program's by a relative error of at most 0.0028.
Values may be sent and summed in bfloat16 or wider, within the bound.
A program may use at most 128 MiB of HBM per device.

v0:
```python
import jax
import jax.numpy as jnp
from jax import lax
from jax.sharding import PartitionSpec as P

COLOUR_CHANNELS = 3
LEVELS = 5
BS = 64
SW = 64
FH = 128
FW = 1024
TILE_DEV = 4


TAPS = (1.0, 4.0, 6.0, 4.0, 1.0)


def as_sent(shard):
    return jax.tree.map(lambda a: a.astype(jnp.bfloat16) if a.dtype == jnp.float32 else a, shard)


def shrink_axis(values, along):
    length = values.shape[along]
    padding = [(0, 0)] * values.ndim
    padding[along] = (2, 2)
    padded = jnp.pad(values, padding, mode="edge")
    total = TAPS[0] * lax.slice_in_dim(padded, 0, length - 1, 2, along)
    for offset in range(1, 5):
        total = total + TAPS[offset] * lax.slice_in_dim(
            padded, offset, offset + length - 1, 2, along
        )
    return total / 16.0


def grow_axis(values, along):
    length = values.shape[along]
    padding = [(0, 0)] * values.ndim
    padding[along] = (1, 1)
    padded = jnp.pad(values, padding, mode="edge")
    before = lax.slice_in_dim(padded, 0, length, 1, along)
    middle = lax.slice_in_dim(padded, 1, length + 1, 1, along)
    after_rows = lax.slice_in_dim(padded, 2, length + 2, 1, along)
    even_rows = (before + 6.0 * middle + after_rows) / 8.0
    odd_rows = (middle + after_rows) / 2.0
    stacked = jnp.stack((even_rows, odd_rows), axis=along + 1)
    new_shape = list(values.shape)
    new_shape[along] = 2 * length
    return stacked.reshape(new_shape)


def shrink(values):
    return shrink_axis(shrink_axis(values, values.ndim - 2), values.ndim - 1)


def grow(values):
    return grow_axis(grow_axis(values, values.ndim - 2), values.ndim - 1)


def gaussian_levels(image):
    levels = [image]
    for level_k in range(LEVELS - 1):
        levels.append(shrink(levels[-1]))
    return levels


def band_levels(image):
    gaussian = gaussian_levels(image)
    return [gaussian[level_k] - grow(gaussian[level_k + 1]) for level_k in range(LEVELS - 1)] + [
        gaussian[-1]
    ]


def frame_strips(bands, cell_index):
    pieces = []
    for level_k in range(LEVELS):
        column_start = cell_index * (16 >> level_k)
        strip_piece = lax.dynamic_slice_in_dim(bands[level_k], column_start, SW >> level_k, 2)
        pieces.append(strip_piece.reshape(-1))
    return jnp.concatenate(pieces).astype(jnp.bfloat16)


def blend_frame(bands, level_weights, mask_levels, cell_index, partner_vec):
    offset_now = 0
    outputs = []
    blocks_high = FH // BS
    blocks_wide = FW // BS
    for level_k in range(LEVELS):
        band_now = bands[level_k]
        column_start = cell_index * (16 >> level_k)
        strip_width = SW >> level_k
        rows_here = FH >> level_k
        count_of_values = COLOUR_CHANNELS * rows_here * strip_width
        remote = (
            partner_vec[offset_now : offset_now + count_of_values]
            .reshape(COLOUR_CHANNELS, rows_here, strip_width)
            .astype(jnp.float32)
        )
        offset_now += count_of_values
        own_strip = lax.dynamic_slice_in_dim(band_now, column_start, strip_width, 2)
        mask_share = mask_levels[level_k][None]
        mixed_band = lax.dynamic_update_slice_in_dim(
            band_now, mask_share * own_strip + (1.0 - mask_share) * remote, column_start, 2
        )
        weights = level_weights[level_k][None]
        stacked = jnp.concatenate((weights * mixed_band, weights), axis=0).astype(jnp.bfloat16)
        block_side = BS >> level_k
        tiled_blocks = stacked.reshape(
            COLOUR_CHANNELS + 1, blocks_high, block_side, blocks_wide, block_side
        ).transpose(1, 3, 0, 2, 4)
        outputs.append(
            tiled_blocks.reshape(
                blocks_high * blocks_wide, COLOUR_CHANNELS + 1, block_side * block_side
            )
        )
    return jnp.concatenate(outputs, axis=2)


def collapse(summed_totals):
    normal = summed_totals[:, :COLOUR_CHANNELS] / jnp.maximum(
        summed_totals[:, COLOUR_CHANNELS:], 1.0
    )
    offset_now = 0
    levels = []
    for level_k in range(LEVELS):
        block_side = BS >> level_k
        levels.append(
            normal[:, :, offset_now : offset_now + block_side * block_side].reshape(
                normal.shape[0], COLOUR_CHANNELS, block_side, block_side
            )
        )
        offset_now += block_side * block_side
    merged = levels[-1]
    for level_k in range(LEVELS - 2, -1, -1):
        merged = levels[level_k] + grow(merged)
    return merged.reshape(merged.shape[0], COLOUR_CHANNELS, BS * BS)


def local(frames, weight_map, seam_mask, strip_cell, partner, tile_group, tile_position_in_group):
    frame_count = frames.shape[0]
    group_count = lax.axis_size("frames")
    tile_parts = lax.axis_size("tiles")
    bands = band_levels(frames.astype(jnp.float32))
    strip_vecs = jax.vmap(frame_strips)(bands, strip_cell)
    partner_group = partner // (tile_parts * frame_count)
    requested_rows = partner_group * frame_count + partner % frame_count
    piece = jax.tree.map(
        lambda part: lax.all_gather(part, "frames", axis=0, tiled=True), as_sent(strip_vecs)
    )
    row_numbers = jnp.arange(piece.shape[0], dtype=jnp.int32)
    select = (row_numbers[None, :] == requested_rows[:, None]).astype(jnp.bfloat16)
    found = jnp.zeros(strip_vecs.shape, jnp.float32) + jnp.dot(
        select, piece, preferred_element_type=jnp.float32
    )
    partner_vecs = found.astype(jnp.bfloat16)
    level_weights = gaussian_levels(weight_map.astype(jnp.float32))
    mask_levels = gaussian_levels(seam_mask.astype(jnp.float32))
    blocks = jax.vmap(blend_frame)(bands, level_weights, mask_levels, strip_cell, partner_vecs)
    rows_total = frame_count * blocks.shape[1]
    flat_blocks = blocks.reshape(rows_total, -1)
    capacity = max(2, (2 * rows_total + group_count - 1) // group_count)
    destination = tile_group.reshape(rows_total)
    group_hot = (destination[:, None] == jnp.arange(group_count, dtype=jnp.int32)[None, :]).astype(
        jnp.int32
    )
    earlier = jnp.cumsum(group_hot, axis=0) - group_hot
    position = jnp.sum(earlier * group_hot, axis=1)
    slot_index = destination * capacity + position
    dispatch = (
        jnp.arange(group_count * capacity, dtype=jnp.int32)[:, None] == slot_index[None, :]
    ).astype(jnp.bfloat16)
    send_blocks = (
        jnp.dot(dispatch, flat_blocks, preferred_element_type=jnp.float32)
        .astype(jnp.bfloat16)
        .reshape(group_count, capacity, -1)
    )
    labels = (tile_position_in_group.reshape(rows_total, 1) + 1).astype(jnp.bfloat16)
    send_labels = (
        jnp.dot(dispatch, labels, preferred_element_type=jnp.float32)
        .astype(jnp.bfloat16)
        .reshape(group_count, capacity)
    )
    got_blocks, got_labels = (
        lax.all_to_all(send_blocks, "frames", split_axis=0, concat_axis=0, tiled=True),
        lax.all_to_all(send_labels, "frames", split_axis=0, concat_axis=0, tiled=True),
    )
    tiles_group = tile_parts * TILE_DEV
    tile_numbers = (jnp.arange(tiles_group, dtype=jnp.int32) + 1).astype(jnp.bfloat16)
    tile_hot = (got_labels.reshape(1, -1) == tile_numbers[:, None]).astype(jnp.bfloat16)
    partial_sums = jnp.dot(
        tile_hot, got_blocks.reshape(group_count * capacity, -1), preferred_element_type=jnp.float32
    ).reshape(tiles_group, COLOUR_CHANNELS + 1, -1)
    owned = lax.psum_scatter(partial_sums, "tiles", scatter_dimension=0, tiled=True)
    return collapse(owned)


def solution(mesh):
    in_specs = (
        P(("frames", "tiles"), None, None, None),
        P(("frames", "tiles"), None, None),
        P(("frames", "tiles"), None, None),
        P(("frames", "tiles")),
        P(("frames", "tiles")),
        P(("frames", "tiles"), None, None),
        P(("frames", "tiles"), None),
    )
    out_specs = P(("frames", "tiles"), None, None)
    return jax.shard_map(local, mesh=mesh, in_specs=in_specs, out_specs=out_specs, check_vma=False)
```

profile of v0, /device:TPU:1, one launch (start us, length us, event | category | flops | bytes accessed | tf_op | source)
XLA Modules:
  0.0 568.6 jit_solution(13972431714507554002)
XLA Ops:
  10.9 13.3 %all-to-all-start = ((bf16[64,1,2]{2,1,0:T(2,128)(2,1)}), bf16[64,1,2]{2,1,0:T(2,128)(2,1)}, u32[]{:S(2)}, u32[]{:S(2)}) async-start(bf16[64,1,2]{2,1,0:T(2,128)(2,1)} %all_to_all.12), calls=%async_computation | async-start | bytes 65536 | tf_op jit(solution)/shard_map/all_to_all | solution.py:184
  25.1 1.3 convert_element_type.184
  27.7 2.2 slice.1145
  29.9 2.1 slice.1144
  32.0 2.1 slice.1143
  34.2 2.0 add_multiply_fusion
  37.1 17.6 %slice.1156 = f32[1,3,64,512]{3,2,1,0:T(8,128)S(1)} slice(f32[1,3,64,1028]{3,2,1,0:T(8,128)S(1)} %concatenate.380), slice={[0:1:1], [0:3:1], [0:64:1], [4:1027:2]} | slice | bytes 786432 | tf_op jit(solution)/shard_map/slice | solution.py:29
  54.7 17.6 %slice.1155 = f32[1,3,64,512]{3,2,1,0:T(8,128)S(1)} slice(f32[1,3,64,1028]{3,2,1,0:T(8,128)S(1)} %concatenate.380), slice={[0:1:1], [0:3:1], [0:64:1], [3:1026:2]} | slice | bytes 786432 | tf_op jit(solution)/shard_map/slice | solution.py:29
  72.3 17.6 %slice.1154 = f32[1,3,64,512]{3,2,1,0:T(8,128)S(1)} slice(f32[1,3,64,1028]{3,2,1,0:T(8,128)S(1)} %concatenate.380), slice={[0:1:1], [0:3:1], [0:64:1], [2:1025:2]} | slice | bytes 786432 | tf_op jit(solution)/shard_map/slice | solution.py:29
  89.9 17.8 %slice.1153 = f32[1,3,64,512]{3,2,1,0:T(8,128)S(1)} slice(f32[1,3,64,1028]{3,2,1,0:T(8,128)S(1)} %concatenate.380), slice={[0:1:1], [0:3:1], [0:64:1], [1:1024:2]} | slice | bytes 786432 | tf_op jit(solution)/shard_map/slice | solution.py:29
  107.8 18.2 %slice.1152 = f32[1,3,64,512]{3,2,1,0:T(8,128)} slice(f32[1,3,64,1028]{3,2,1,0:T(8,128)S(1)} %concatenate.380), slice={[0:1:1], [0:3:1], [0:64:1], [0:1023:2]} | slice | bytes 786432 | tf_op jit(solution)/shard_map/slice | solution.py:27
  126.0 1.2 broadcast_multiply_fusion
  129.5 3.3 slice.1183
  132.8 3.3 slice.1182
  136.1 3.3 slice.1181
  139.4 3.3 slice.1180
  142.7 3.5 slice.1179
  162.3 4.7 multiply_bitcast_fusion.1
  167.0 1.4 pad_maximum_fusion.1
  168.4 1.5 copy.552
  169.9 1.6 copy.553
  171.6 1.8 convert_subtract_fusion
  192.5 1.3 add_multiply_fusion.1
  194.3 4.5 slice.1258
  198.8 4.9 slice.1257
  203.7 4.5 slice.1256
  208.2 4.5 slice.1255
  212.7 5.2 slice.1254
  219.8 1.1 slice.1298
  220.9 1.1 slice.1297
  222.1 1.1 slice.1296
  223.3 1.1 slice.1295
  224.5 1.1 slice.1294
  236.7 2.5 and_reduce_fusion.4
  239.2 4.6 and_reduce_fusion
  243.8 4.5 and_reduce_fusion.2
  248.2 10.9 %all-gather.3.cloned.1.call-done = bf16[64,1,32736]{2,1,0:T(2,128)(2,1)} async-done(((bf16[1,1,32736]{2,1,0:T(2,128)(2,1)}), bf16[64,1,32736]{2,1,0:T(2,128)(2,1)}) %all-gather.3.cloned.1.call-update) | async-done | bytes 4190224 | tf_op jit(solution)/shard_map/all_gather | solution.py:147
  259.2 7.9 %fusion = f32[1,32736]{1,0:T(1,128)S(1)} fusion(bf16[64,1,32736]{2,1,0:T(2,128)(2,1)} %all-gather.3.cloned.1.call-done, s32[]{:T(128)} %bitcast.18), kind=kOutput, calls=%fused_computation.2 | convolution fusion | flops 4190272 | bytes 4321156 | tf_op jit(solution)/shard_map/dot_general | solution.py:151
  267.7 1.3 dynamic-slice_select_fusion.4
  270.2 1.3 dynamic-slice_select_fusion.3
  271.5 1.5 scatter.21
  273.1 1.5 dynamic-slice_select_fusion.2
  274.5 1.4 scatter.20
  276.0 1.4 dynamic-slice_select_fusion.1
  277.4 1.6 scatter.19
  280.4 1.3 dynamic-slice_select_fusion
  281.7 1.9 scatter.16
  287.1 1.2 maximum_bitcast_fusion.1
  292.4 1.7 reshape.1245
  296.5 4.0 convolution_convert_fusion
  300.5 8.2 %copy.585 = bf16[128,21824]{1,0:T(8,128)(2,1)} copy(bf16[128,21824]{0,1:T(8,128)(2,1)} %convolution_convert_fusion) | data formatting | bytes 11173888 | tf_op jit(solution)/shard_map/convert_element_type | solution.py:173
  308.7 8.2 %reshape.1299 = bf16[64,2,21824]{2,1,0:T(2,128)(2,1)} reshape(bf16[128,21824]{1,0:T(8,128)(2,1)} %copy.585) | data formatting | bytes 11173888 | tf_op jit(solution)/shard_map/reshape | solution.py:174
  316.9 6.5 %all-to-all-start.1 = ((bf16[64,2,21824]{2,1,0:T(2,128)(2,1)}), bf16[64,2,21824]{2,1,0:T(2,128)(2,1)}, u32[]{:S(2)}, u32[]{:S(2)}) async-start(bf16[64,2,21824]{2,1,0:T(2,128)(2,1)} %reshape.1299), calls=%async_computation.1 | async-start | bytes 11206656 | tf_op jit(solution)/shard_map/all_to_all | solution.py:183
  324.5 125.0 %all-to-all-done.1 = bf16[64,2,21824]{2,1,0:T(2,128)(2,1)} async-done(((bf16[64,2,21824]{2,1,0:T(2,128)(2,1)}), bf16[64,2,21824]{2,1,0:T(2,128)(2,1)}, u32[]{:S(2)}, u32[]{:S(2)}) %all-to-all-start.1) | async-done | bytes 5586976 | tf_op jit(solution)/shard_map/all_to_all | solution.py:183
  449.6 8.8 %reshape.1300 = bf16[128,21824]{1,0:T(8,128)(2,1)} reshape(bf16[64,2,21824]{2,1,0:T(2,128)(2,1)} %all-to-all-done.1) | data formatting | bytes 11173888 | tf_op jit(solution)/shard_map/reshape | solution.py:190
  458.4 8.3 %copy.586 = bf16[21824,128]{1,0:T(8,128)(2,1)} copy(bf16[21824,128]{0,1:T(8,128)(2,1)} %bitcast.257) | data formatting | bytes 11173888 | tf_op jit(solution)/shard_map/dot_general | solution.py:189
  466.7 5.4 fusion.92
  473.3 48.4 %all-reduce.8.cloned.1.call-done = f32[16,4,5456]{2,0,1:T(8,128)} async-done(((f32[16,4,5456]{2,0,1:T(8,128)}), f32[16,4,5456]{2,0,1:T(8,128)}) %all-reduce.8.cloned.1.call-update) | async-done | bytes 1396752
  524.6 4.8 copy.588
  529.4 4.0 broadcast_divide_fusion
  533.4 3.2 copy-done
  541.7 6.8 %copy.616 = f32[4,3,64,32,2]{0,4,3,2,1:T(2,128)} copy(f32[4,3,64,32,2]{3,2,1,0,4:T(8,128)S(1)} %pad_maximum_fusion.5) | data formatting | bytes 393216 | tf_op jit(solution)/shard_map/stack | solution.py:45
  548.5 7.8 %slice_add_fusion = f32[4,3,4096]{0,2,1:T(8,128)} fusion(f32[4,3,4096]{0,2,1:T(8,128)} %bitcast.256, f32[4,3,5456]{0,2,1:T(8,128)} %copy-done), kind=kLoop, calls=%fused_computation.1 | loop fusion | flops 49152 | bytes 589824 | tf_op jit(solution)/shard_map/add | solution.py:134
  556.3 5.1 copy.617
  (482 shorter events, 78.1 us)
Async XLA Ops:
  8.8 0.5 copy-start.28
  10.9 306.0 %all-to-all-start = ((bf16[64,1,2]{2,1,0:T(2,128)(2,1)}), bf16[64,1,2]{2,1,0:T(2,128)(2,1)}, u32[]{:S(2)}, u32[]{:S(2)}) async-start(bf16[64,1,2]{2,1,0:T(2,128)(2,1)} %all_to_all.12), calls=%async_computation | async-start | bytes 65536 | tf_op jit(solution)/shard_map/all_to_all | solution.py:184
  24.2 234.9 %all-gather.3.cloned.1.call-start = ((), (), s32[]{:S(2)}) async-start(), calls=%async_computation.2 | async-start | bytes 8519680 | tf_op jit(solution)/shard_map/all_gather | solution.py:147
  155.1 0.6 copy-start.6
  156.2 2.4 copy-start.4
  171.6 2.2 copy-start.17
  171.6 2.3 copy-start.21
  171.6 2.3 copy-start.35
  171.6 3.7 copy-start.15
  173.4 14.4 %copy-start.3 = (bf16[1,128,1024]{2,1,0:T(8,128)(2,1)S(1)}, bf16[1,128,1024]{2,1,0:T(8,128)(2,1)}, u32[]{:S(2)}) copy-start(bf16[1,128,1024]{2,1,0:T(8,128)(2,1)} %param.18) | copy-start | bytes 786436
  173.9 0.7 copy-start.8
  182.3 6.8 %copy-start.10 = (f32[1,32,16]{1,2,0:T(8,128)}, f32[1,32,16]{1,2,0:T(8,128)S(1)}, u32[]{:S(2)}) copy-start(f32[1,32,16]{1,2,0:T(8,128)S(1)} %get-tuple-element.153) | copy-start | bytes 6148
  218.9 10.2 %copy-start.16 = (s32[1,128,64]{1,2,0:T(8,128)S(1)}, s32[1,128,64]{1,2,0:T(8,128)}, u32[]{:S(2)}) copy-start(s32[1,128,64]{1,2,0:T(8,128)} %param.19) | copy-start | bytes 98308
  219.0 10.3 %copy-start.23 = (f32[1,8,4]{1,2,0:T(4,128)S(1)}, f32[1,8,4]{1,2,0:T(4,128)}, u32[]{:S(2)}) copy-start(f32[1,8,4]{1,2,0:T(4,128)} %slice.1399) | copy-start | bytes 388
  219.0 10.3 %copy-start.24 = (f32[1,8,4]{1,2,0:T(4,128)S(1)}, f32[1,8,4]{1,2,0:T(4,128)}, u32[]{:S(2)}) copy-start(f32[1,8,4]{1,2,0:T(4,128)} %slice.1398) | copy-start | bytes 388
  219.0 10.3 %copy-start.25 = (f32[1,8,4]{1,2,0:T(4,128)S(1)}, f32[1,8,4]{1,2,0:T(4,128)}, u32[]{:S(2)}) copy-start(f32[1,8,4]{1,2,0:T(4,128)} %slice.1397) | copy-start | bytes 388
  219.0 10.3 %copy-start.26 = (f32[1,8,4]{1,2,0:T(4,128)S(1)}, f32[1,8,4]{1,2,0:T(4,128)}, u32[]{:S(2)}) copy-start(f32[1,8,4]{1,2,0:T(4,128)} %slice.1396) | copy-start | bytes 388
  219.0 10.3 %copy-start.27 = (f32[1,8,4]{1,2,0:T(4,128)S(1)}, f32[1,8,4]{1,2,0:T(4,128)}, u32[]{:S(2)}) copy-start(f32[1,8,4]{1,2,0:T(4,128)} %slice.1395) | copy-start | bytes 388
  219.0 10.5 %copy-start.22 = (f32[16,8]{0,1:T(8,128)S(1)}, f32[16,8]{0,1:T(8,128)}, u32[]{:S(2)}) copy-start(f32[16,8]{0,1:T(8,128)} %get-tuple-element.148) | copy-start | bytes 1540
  219.0 11.2 %copy-start.20 = (f32[32,16]{0,1:T(8,128)S(1)}, f32[32,16]{0,1:T(8,128)}, u32[]{:S(2)}) copy-start(f32[32,16]{0,1:T(8,128)} %get-tuple-element.152) | copy-start | bytes 6148
  219.0 11.3 %copy-start.11 = (f32[1,32,16]{1,2,0:T(8,128)S(1)}, f32[1,32,16]{1,2,0:T(8,128)}, u32[]{:S(2)}) copy-start(f32[1,32,16]{1,2,0:T(8,128)} %copy-done.10) | copy-start | bytes 6148
  219.0 11.4 %copy-start.18 = (f32[64,32]{0,1:T(8,128)S(1)}, f32[64,32]{0,1:T(8,128)}, u32[]{:S(2)}) copy-start(f32[64,32]{0,1:T(8,128)} %get-tuple-element.156) | copy-start | bytes 24580
  219.0 11.5 %copy-start.14 = (f32[128,64]{0,1:T(8,128)S(1)}, f32[128,64]{0,1:T(8,128)}, u32[]{:S(2)}) copy-start(f32[128,64]{0,1:T(8,128)} %get-tuple-element.233) | copy-start | bytes 98308
  223.2 9.9 %copy-start.41 = (s32[1,3]{1,0:T(1,128)S(1)}, s32[1,3]{1,0:T(1,128)}, u32[]{:S(2)}) copy-start(s32[1,3]{1,0:T(1,128)} %constant.374.clone.1) | copy-start | bytes 40
  223.2 10.6 %copy-start.40 = (s32[1,3]{1,0:T(1,128)S(1)}, s32[1,3]{1,0:T(1,128)}, u32[]{:S(2)}) copy-start(s32[1,3]{1,0:T(1,128)} %constant.372.clone.1) | copy-start | bytes 40
  223.2 11.3 %copy-start.39 = (s32[1,3]{1,0:T(1,128)S(1)}, s32[1,3]{1,0:T(1,128)}, u32[]{:S(2)}) copy-start(s32[1,3]{1,0:T(1,128)} %constant.370.clone.1) | copy-start | bytes 40
  223.2 12.0 %copy-start.38 = (s32[1,3]{1,0:T(1,128)S(1)}, s32[1,3]{1,0:T(1,128)}, u32[]{:S(2)}) copy-start(s32[1,3]{1,0:T(1,128)} %constant.368.clone.1) | copy-start | bytes 40
  223.2 12.7 %copy-start.37 = (s32[1,3]{1,0:T(1,128)S(1)}, s32[1,3]{1,0:T(1,128)}, u32[]{:S(2)}) copy-start(s32[1,3]{1,0:T(1,128)} %constant.354.clone.1) | copy-start | bytes 40
  223.3 13.4 %copy-start.30 = (s32[4]{0:T(128)S(1)}, s32[4]{0:T(128)}, u32[]{:S(2)}) copy-start(s32[4]{0:T(128)} %constant.355.clone.1) | copy-start | bytes 52
  224.4 14.8 %copy-start.33 = (s32[4]{0:T(128)S(1)}, s32[4]{0:T(128)}, u32[]{:S(2)}) copy-start(s32[4]{0:T(128)} %constant.375.clone.1) | copy-start | bytes 52
  224.4 14.7 %copy-start.34 = (s32[4]{0:T(128)S(1)}, s32[4]{0:T(128)}, u32[]{:S(2)}) copy-start(s32[4]{0:T(128)} %constant.373.clone.1) | copy-start | bytes 52
  224.4 19.3 %copy-start.31 = (s32[4]{0:T(128)S(1)}, s32[4]{0:T(128)}, u32[]{:S(2)}) copy-start(s32[4]{0:T(128)} %constant.371.clone.1) | copy-start | bytes 52
  224.5 19.3 %copy-start.32 = (s32[4]{0:T(128)S(1)}, s32[4]{0:T(128)}, u32[]{:S(2)}) copy-start(s32[4]{0:T(128)} %constant.369.clone.1) | copy-start | bytes 52
  259.2 11.1 %copy-start.7 = (f32[1,3,16,128]{3,2,1,0:T(8,128)S(1)}, f32[1,3,16,128]{3,2,1,0:T(8,128)}, u32[]{:S(2)}) copy-start(f32[1,3,16,128]{3,2,1,0:T(8,128)} %copy-done.6) | copy-start | bytes 73732
  259.2 11.1 %copy-start.19 = (f32[16,8]{1,0:T(8,128)S(1)}, f32[16,8]{1,0:T(8,128)}, u32[]{:S(2)}) copy-start(f32[16,8]{1,0:T(8,128)} %copy.574) | copy-start | bytes 1540
  259.2 13.9 %copy-start.5 = (f32[1,3,32,256]{3,2,1,0:T(8,128)S(1)}, f32[1,3,32,256]{3,2,1,0:T(8,128)}, u32[]{:S(2)}) copy-start(f32[1,3,32,256]{3,2,1,0:T(8,128)} %copy-done.4) | copy-start | bytes 294916
  288.2 1.4 copy-start.1
  290.9 1.0 copy-start.2
  292.4 1.7 copy-start.9
  292.4 1.7 copy-start.12
  292.4 1.7 copy-start.13
  295.3 1.1 copy-start.29
  316.9 132.6 %all-to-all-start.1 = ((bf16[64,2,21824]{2,1,0:T(2,128)(2,1)}), bf16[64,2,21824]{2,1,0:T(2,128)(2,1)}, u32[]{:S(2)}, u32[]{:S(2)}) async-start(bf16[64,2,21824]{2,1,0:T(2,128)(2,1)} %reshape.1299), calls=%async_computation.1 | async-start | bytes 11206656 | tf_op jit(solution)/shard_map/all_to_all | solution.py:183
  323.4 198.2 %all-reduce.8.cloned.1.call-start = ((), (), s32[]{:S(2)}) async-start(), calls=%async_computation.3 | async-start | bytes 2818048
  466.7 5.4 copy-start.36
  533.4 3.2 copy-start
Sparse Core Ops, SparseCore 0:
  174.7 84.4 all-gather.2
  472.2 49.4 all-reduce.7
where the time goes:
time: 579 us; the launch traced here: 569 us
  local copies, waits for them, and re-layouts  268 us (46%)
  waiting for transfers between devices  184 us (32%)
  other arithmetic  60.4 us (10%)
  starting transfers between devices  20 us (3%)
  between operations  18.3 us (3%)
  matrix products  18.1 us (3%)
    slice x96, local copies, waits for them, and re-layouts, shrink_axis(): lax.slice_in_dim(padded, offset, offset + length - 1, 2, along)  129 us
    all_to_all x1, waiting for transfers between devices, local(): lax.all_to_all(send_blocks, 'frames', split_axis=0, concat_axis=0, tiled=...  125 us
    unnamed x3, waiting for transfers between devices  48.4 us
    slice x24, local copies, waits for them, and re-layouts, shrink_axis(): total = TAPS[0] * lax.slice_in_dim(padded, 0, length - 1, 2, along)  34.9 us
    another operation x17, other arithmetic  19.6 us
    all_to_all x1, starting transfers between devices, local(): lax.all_to_all(send_labels, 'frames', split_axis=0, concat_axis=0, tiled=...  13.3 us
  transfers between devices with their start and end apart: 4, of which 3 were waited for; matrix products, arithmetic and copies ran while one was open for 49% of the time, Pallas kernels for 0%

commit v1 on v0

v1 whole, which is shorter than its diff:
```python
import functools

import jax
import jax.numpy as jnp
import numpy as np
from jax import lax
from jax.experimental import pallas as pl
from jax.experimental.pallas import tpu as pltpu
from jax.sharding import PartitionSpec as P

F32 = jnp.float32
BF16 = jnp.bfloat16
I32 = jnp.int32
AXES = ("frames", "tiles")
DEV = 256
ROWS = 24
TILES = 1024
GROUPS = 64


def iota(shape, axis):
    return lax.broadcasted_iota(I32, shape, axis)


def dot(a, b):
    return jnp.dot(a, b, preferred_element_type=F32)


def dot_t(a, b):
    return lax.dot_general(a, b, (((1,), (1,)), ((), ())), preferred_element_type=F32)


def tap5(a, b, c, d, e):
    return (a + e) * (1.0 / 16.0) + (b + d) * 0.25 + c * 0.375


def encode_kernel(cell_ref, frames_ref, weight_ref, mask_ref, out_ref, perm, zbuf, lev0, half, tail, *levs):
    cell = cell_ref[0]
    sub = iota((8, 128), 0)
    lane = iota((8, 128), 1)
    grp = lane % 64
    low = lane < 64
    top = (sub == 0) & low
    bottom = (sub == 7) & (lane >= 64)

    def prev(v):
        t = pltpu.roll(v, 1, 0)
        return jnp.where(sub == 0, pltpu.roll(t, 64, 1), t)

    def following(v):
        t = pltpu.roll(v, 7, 0)
        return jnp.where(sub == 7, pltpu.roll(t, 64, 1), t)

    def left(v, first, clamp):
        return jnp.where(first, clamp, pltpu.roll(v, 1, 1))

    def right(v, last, clamp):
        return jnp.where(last, clamp, pltpu.roll(v, 127, 1))

    def get(img, k, r, a):
        return lev0[img, r, a] if k == 0 else levs[k - 1][img, r, a]

    def shrink_level(img, k, first, last):
        rows, cols = 8 >> k, 16 >> k
        if rows > 1:
            for a in range(cols):
                v = [get(img, k, r, a) for r in range(rows)]
                m2 = jnp.where(top, v[0], prev(v[rows - 2]))
                m1 = jnp.where(top, v[0], prev(v[rows - 1]))
                p1 = jnp.where(bottom, v[rows - 1], following(v[0]))
                w = [m2, m1] + v + [p1]
                for r in range(rows // 2):
                    half[r, a] = tap5(*w[2 * r : 2 * r + 5])
            out_rows = rows // 2
        else:
            for a in range(cols):
                v = get(img, k, 0, a)
                m1 = jnp.where(top, v, prev(v))
                m2 = jnp.where(top, v, prev(m1))
                p1 = jnp.where(bottom, v, following(v))
                p2 = jnp.where(bottom, v, following(p1))
                half[0, a] = tap5(m2, m1, v, p1, p2)
            out_rows = 1
        for r in range(out_rows):
            v = [half[r, a] for a in range(cols)]
            m2 = left(v[cols - 2], first, v[0])
            m1 = left(v[cols - 1], first, v[0])
            p1 = right(v[0], last, v[cols - 1])
            w = [m2, m1] + v + [p1]
            for a in range(cols // 2):
                levs[k][img, r, a] = tap5(*w[2 * a : 2 * a + 5])

    def grow_to_half(img, k, first, last):
        cols = 16 >> (k + 1)
        if k == 3:
            for a in range(cols):
                v = get(img, 4, 0, a)
                p1, n1 = prev(v), following(v)
                p2, n2 = prev(p1), following(n1)
                up = jnp.where(top, v, p2)
                down = jnp.where((sub == 6) & (lane >= 64), v, n2)
                even = (up + down) * 0.125 + v * 0.75
                odd = (p1 + jnp.where(bottom, p1, n1)) * 0.5
                half[0, a] = jnp.where(sub % 2 == 0, even, odd)
            return
        rows = 8 >> (k + 1)
        for a in range(cols):
            v = [get(img, k + 1, r, a) for r in range(rows)]
            w = [jnp.where(top, v[0], prev(v[rows - 1]))] + v + [jnp.where(bottom, v[rows - 1], following(v[0]))]
            for r in range(rows):
                half[2 * r, a] = (w[r] + w[r + 2]) * 0.125 + w[r + 1] * 0.75
                half[2 * r + 1, a] = (w[r + 1] + w[r + 2]) * 0.5

    kap = iota((1024, 1), 0)
    nu = iota((1, 1024), 1)
    perm[...] = (kap == (nu % 64) * 16 + nu // 64).astype(F32).astype(BF16)
    ri, ci = iota((128, 128), 0), iota((128, 128), 1)
    order = ((ri // 8 % 2) * 64 + (ri % 8) * 8 + ri // 16 == ci).astype(F32).astype(BF16)

    def place(img):
        for r in range(8):
            for pair in range(8):
                z0 = zbuf[r * 16 : r * 16 + 8, pair * 128 : pair * 128 + 128]
                z1 = zbuf[r * 16 + 8 : r * 16 + 16, pair * 128 : pair * 128 + 128]
                lev0[img, r, 2 * pair] = jnp.where(low, z0, pltpu.roll(z1, 64, 1))
                lev0[img, r, 2 * pair + 1] = jnp.where(low, pltpu.roll(z0, 64, 1), z1)

    for img in range(4):
        x = frames_ref[0, img] if img < 3 else weight_ref[0]
        zbuf[...] = dot(dot(order, x).astype(BF16), perm[...])
        place(img)
    km = iota((64, 1), 0)
    strip_perm = ((km % 16 == nu // 64) & (nu % 64 == cell + km // 16)).astype(F32).astype(BF16)
    zbuf[...] = dot(dot(order, mask_ref[0].astype(F32).astype(BF16)).astype(BF16), strip_perm)
    place(4)

    first, last = grp == 0, grp == 63
    mfirst, mlast = grp == cell, grp == cell + 3
    for k in range(4):
        for img in range(4):
            shrink_level(img, k, first, last)
        shrink_level(4, k, mfirst, mlast)

    strip = (grp >= cell) & (grp < cell + 4)
    kp, np_ = iota((128, 128), 0), iota((128, 128), 1)
    pick = (kp == (np_ // 4 % 2) * 64 + cell + np_ % 4).astype(F32).astype(BF16)
    slot = lane // 8

    tail[...] = jnp.zeros(tail.shape, F32)

    def products(k, r, a, bands):
        w, m = get(3, k, r, a), get(4, k, r, a)
        own = w * jnp.where(strip, m, 1.0)
        q = w * (1.0 - m)
        data = [own * b for b in bands] + [w]
        picked = dot(jnp.concatenate([bands[0], bands[1], bands[2], q], axis=0).astype(BF16), pick)
        return data, [picked[8 * i : 8 * i + 8] for i in range(4)]

    for k in range(4, -1, -1):
        rows, cols = max(8 >> k, 1), 16 >> k
        if k < 4:
            for img in range(3):
                grow_to_half(img, k, first, last)
                for r in range(rows):
                    v = [half[r, a] for a in range(cols // 2)]
                    n = cols // 2
                    w = [left(v[n - 1], first, v[0])] + v + [right(v[0], last, v[n - 1])]
                    for a in range(n):
                        even = (w[a] + w[a + 2]) * 0.125 + w[a + 1] * 0.75
                        odd = (w[a + 1] + w[a + 2]) * 0.5
                        for e, grown in ((0, even), (1, odd)):
                            if k == 0:
                                lev0[img, r, 2 * a + e] = lev0[img, r, 2 * a + e] - grown
                            else:
                                zbuf[img * 32 + r * 8 : img * 32 + r * 8 + 8, (2 * a + e) * 128 : (2 * a + e) * 128 + 128] = (
                                    get(img, k, r, 2 * a + e) - grown
                                )
        for r in range(rows):
            for a in range(cols):
                if k == 0:
                    bands = [lev0[i, r, a] for i in range(3)]
                elif k == 4:
                    bands = [get(i, 4, 0, 0) for i in range(3)]
                else:
                    bands = [zbuf[i * 32 + r * 8 : i * 32 + r * 8 + 8, a * 128 : a * 128 + 128] for i in range(3)]
                data, picked = products(k, r, a, bands)
                if k == 0:
                    c = r * 16 + a
                    rolled = [pltpu.roll(d, 4, 0) for d in data]
                    quarter = sub < 4
                    for h in range(2):
                        parts = []
                        for i in (0, 2):
                            if h == 0:
                                parts.append(jnp.where(quarter, data[i], rolled[i + 1]))
                            else:
                                parts.append(jnp.where(quarter, rolled[i], data[i + 1]))
                        out_ref[2 * c + h, 0:16, :] = jnp.concatenate(parts, axis=0).astype(BF16)
                    u = jnp.zeros((8, 128), F32)
                    for i in range(4):
                        u = jnp.where(slot == i * 4 + sub % 4, picked[i], u)
                    u = u + pltpu.roll(u, 7, 0)
                    u = u + pltpu.roll(u, 6, 0)
                    tail[pl.ds((2 * c) * 8 + 6, 1), :] = u[0:1]
                    tail[pl.ds((2 * c + 1) * 8 + 6, 1), :] = u[4:5]
                elif k == 1:
                    base = (r * 8 + a) * 64
                    for i in range(4):
                        tail[pl.ds(base + i, 8, stride=8), :] = data[i]
                    u = jnp.zeros((8, 128), F32)
                    for i in range(4):
                        u = jnp.where(slot == i, picked[i], u)
                    u = jnp.where(low, u, (cell % 4).astype(F32))
                    old = tail[pl.ds(base + 7, 8, stride=8), :]
                    tail[pl.ds(base + 7, 8, stride=8), :] = old + u
                else:
                    c = {2: r * 4 + a, 3: 8 + a, 4: 10}[k]
                    for p in range(2):
                        base = (p * 128 + c * 8) * 8
                        for e in range(2):
                            tail[pl.ds(base + 4 + e, 8, stride=8), :] = data[2 * p + e]
                        u = jnp.where(slot == 4, picked[2 * p], 0.0)
                        if p == 0:
                            u = jnp.where(slot == 5, picked[1], u)
                        u = jnp.where(slot == 6, picked[3], u)
                        tail[pl.ds(base + 7, 8, stride=8), :] = u
    for d in range(DEV):
        out_ref[d, 16:24, :] = tail[d * 8 : d * 8 + 8, :].astype(BF16)


def encode(cell, frames, weight, mask):
    vmem = pl.BlockSpec(memory_space=pltpu.VMEM)
    return pl.pallas_call(
        encode_kernel,
        out_shape=jax.ShapeDtypeStruct((DEV, ROWS, 128), BF16),
        in_specs=[pl.BlockSpec(memory_space=pltpu.SMEM), vmem, vmem, vmem],
        out_specs=vmem,
        scratch_shapes=[
            pltpu.VMEM((1024, 1024), BF16),
            pltpu.VMEM((128, 1024), F32),
            pltpu.VMEM((5, 8, 16, 8, 128), F32),
            pltpu.VMEM((8, 16, 8, 128), F32),
            pltpu.VMEM((DEV * 8, 128), F32),
        ]
        + [pltpu.VMEM((5, max(8 >> k, 1), 16 >> k, 8, 128), F32) for k in range(1, 5)],
        compiler_params=pltpu.CompilerParams(vmem_limit_bytes=48 << 20),
        name="encode",
    )(cell, frames, weight, mask)


def merge_kernel(ids_ref, sids_ref, partner_ref, msg_ref, out_ref, table, tail, acc):
    lane = iota((8, 128), 1)
    bit1, bit0 = lane // 2 % 2 == 0, lane % 2 == 0
    zero8 = jnp.zeros((8, 128), F32)

    def swap(a, b, keep, by):
        return (
            jnp.where(keep, a, pltpu.roll(b, by, 1)),
            jnp.where(keep, pltpu.roll(a, 128 - by, 1), b),
        )

    @pl.loop(0, GROUPS)
    def _(j):
        x = [msg_ref[4 * j + s].astype(F32) for s in range(4)]
        for s in range(4):
            tail[4 * j + s] = x[s][16:24]
        parts = [[], [], [], []]
        for t in range(3):
            v = [x[s][8 * t : 8 * t + 8] for s in range(4)]
            v[0], v[2] = swap(v[0], v[2], bit1, 2)
            v[1], v[3] = swap(v[1], v[3], bit1, 2)
            v[0], v[1] = swap(v[0], v[1], bit0, 1)
            v[2], v[3] = swap(v[2], v[3], bit0, 1)
            for g in range(4):
                parts[g].append(v[g])
        for g in range(4):
            table[j, g * 32 : g * 32 + 32, :] = jnp.concatenate(parts[g] + [zero8], axis=0).astype(BF16)

    fr = iota((DEV, DEV), 0)
    swap_rows = (fr == partner_ref[...]).astype(F32).astype(BF16)
    p0 = tail[:, 6, :]
    p1 = tail[:, 7, :]
    ln = iota((DEV, 128), 1)
    s0 = dot(swap_rows, p0.astype(BF16))
    s1 = dot(swap_rows, p1.astype(BF16))
    q0 = jnp.where(
        ln < 32,
        pltpu.roll(p0, 32, 1),
        jnp.where(ln < 64, pltpu.roll(p0, 64, 1), jnp.where(ln < 96, pltpu.roll(p0, 96, 1), 0.0)),
    )
    sl = ln // 8
    q1 = jnp.where(
        sl == 0,
        pltpu.roll(p1, 104, 1),
        jnp.where(
            (sl == 1) | (sl == 4),
            pltpu.roll(p1, 112, 1),
            jnp.where((sl == 2) | (sl == 5), pltpu.roll(p1, 120, 1), 0.0),
        ),
    )
    shift = jnp.where(ln < 64, pltpu.roll(p1, 64, 1), p1)

    def turn(c):
        result = c
        for by in (1, 2, 3):
            turned = jnp.where(ln % 4 >= by, pltpu.roll(c, by, 1), pltpu.roll(c, 124 + by, 1))
            result = jnp.where(shift == float(by), turned, result)
        return result

    both = jnp.concatenate([turn(q0 * s0), turn(q1 * s1)], axis=1).astype(BF16)
    kq, nq = iota((256, 1), 0), iota((1, 1024), 1)
    target = jnp.where(nq // 32 % 4 == nq // 128 % 4, (nq % 32) * 8 + nq // 128, -1)
    extra = dot(both, (kq == target).astype(F32).astype(BF16)).astype(BF16)

    tile = iota((TILES, 256), 0)
    acc[...] = jnp.zeros((TILES, 128), F32)
    for s in range(8):
        hot = (tile == sids_ref[s : s + 1, :]).astype(F32).astype(BF16)
        acc[...] += dot(hot, extra[:, s * 128 : s * 128 + 128])

    @pl.loop(0, GROUPS // 4)
    def _(j):
        hots, datas = [], []
        for s in range(4):
            row = ids_ref[pl.ds(4 * j + s, 1), :]
            hots.append((iota((TILES, 128), 0) == row).astype(F32).astype(BF16))
            datas.append(table[4 * j + s])
        acc[...] += dot_t(jnp.concatenate(hots, axis=1), jnp.concatenate(datas, axis=1))

    sums = acc[...]
    ln = iota((TILES, 128), 1)
    r = ln % 32
    den = jnp.ones((TILES, 128), F32)
    for low, high, by in ((0, 4, 12), (4, 8, 8), (8, 12, 4), (16, 17, 3), (17, 18, 2), (18, 19, 1)):
        den = jnp.where((r >= low) & (r < high), pltpu.roll(sums, 128 - by, 1), den)
    out_ref[...] = (sums / jnp.maximum(den, 1.0)).astype(BF16)


def merge(ids, sids, partner, msg):
    vmem = pl.BlockSpec(memory_space=pltpu.VMEM)
    return pl.pallas_call(
        merge_kernel,
        out_shape=jax.ShapeDtypeStruct((TILES, 128), BF16),
        in_specs=[vmem] * 4,
        out_specs=vmem,
        scratch_shapes=[
            pltpu.VMEM((GROUPS, 128, 128), BF16),
            pltpu.VMEM((DEV, 8, 128), F32),
            pltpu.VMEM((TILES, 128), F32),
        ],
        compiler_params=pltpu.CompilerParams(vmem_limit_bytes=48 << 20),
        name="merge",
    )(ids, sids, partner, msg)


def grow_matrices():
    gammas = [np.eye(64)]
    for k in range(4):
        n = 32 >> k
        g = np.zeros((2 * n, n))
        for i in range(n):
            for j, v in ((i - 1, 0.125), (i, 0.75), (i + 1, 0.125)):
                g[2 * i, min(max(j, 0), n - 1)] += v
            for j in (i, i + 1):
                g[2 * i + 1, min(j, n - 1)] += 0.5
        gammas.append(gammas[-1] @ g)
    return gammas


def collapse_tables():
    gam = grow_matrices()
    d = np.arange(256)
    h, a0, r0 = d % 2, d // 2 % 16, d // 32
    rs1, a1, r1 = d % 8, d // 8 % 8, d // 64
    pic = np.concatenate([np.arange(0, 64, 2), np.arange(1, 64, 2)])
    lead0 = np.zeros((64, 4, 256), np.float32)
    for j in range(4):
        row = (h * 4 + j) * 8 + r0
        lead0[:, j, :] = pic[:, None] == row[None, :]
    lead1 = gam[1][pic][:, rs1 * 4 + r1].astype(np.float32)
    wide1 = np.zeros((256, 4, 64), np.float32)
    for g in range(4):
        wide1[:, g, :] = gam[1][:, g * 8 + a1].T
    lead2 = np.zeros((64, 128), np.float32)
    wide2 = np.zeros((128, 4, 64), np.float32)
    for p in range(88):
        c, rs = p // 8, p % 8
        if c < 8:
            k, row, col, step = 2, rs * 2 + c // 4, c % 4, 4
        elif c < 10:
            k, row, col, step = 3, rs, c - 8, 2
        elif rs % 2 == 0:
            k, row, col, step = 4, rs // 2, 0, 1
        else:
            continue
        lead2[:, p] = gam[k][pic, row]
        for g in range(4):
            wide2[p, g, :] = gam[k][:, g * step + col]
    wide1 = np.tile(wide1, (1, 1, 4)).astype(np.float32)
    wide2 = np.tile(wide2, (1, 1, 4)).astype(np.float32)
    lead2_high = lead2.astype(jnp.bfloat16)
    lead2_low = (lead2 - lead2_high.astype(np.float32)).astype(jnp.bfloat16)
    lane, nu = np.arange(128)[:, None], np.arange(1024)[None, :]
    ch, col, j = nu % 256 // 64, nu % 64, nu // 256
    spread0 = ((lane == (col // 16) * 32 + ch * 4 + j) & (ch < 3)).astype(jnp.bfloat16)
    spread1 = ((lane == j * 32 + 16 + ch) & (ch < 3)).astype(jnp.bfloat16)
    spread2 = ((lane == j * 32 + 20 + ch) & (ch < 3)).astype(jnp.bfloat16)
    keep0 = (a0[:, None] == np.arange(256)[None, :] % 16).astype(np.float32)
    return (
        lead0.reshape(64, 1024).astype(jnp.bfloat16),
        lead1.astype(jnp.bfloat16),
        np.concatenate([lead2_high, lead2_low], axis=0),
        spread0,
        spread1,
        spread2,
        keep0,
        wide1.reshape(256, 1024),
        wide2.reshape(128, 1024),
    )


def split(x):
    high = x.astype(BF16)
    return high, (x - high.astype(F32)).astype(BF16)


def collapse_kernel(
    msg_ref, lead0, lead1, lead2, spread0, spread1, spread2, keep0, wide1, wide2, out_ref, buf, pic
):
    buf[...] = msg_ref[...].astype(F32)
    ln = iota((128, 128), 1)
    low = iota((32, 128), 1) < 64
    for t in range(4):
        x = buf[pl.ds(t, 256, stride=4), :]
        xb = x.astype(BF16)
        fine = dot(xb, spread0[...])
        total = jnp.zeros((64, 256), F32)
        for j in range(4):
            part = (fine[:, j * 256 : j * 256 + 256] * keep0[...]).astype(BF16)
            total = total + dot(lead0[:, j * 256 : j * 256 + 256], part)
        mid = dot(xb, spread1[...]) * wide1[...]
        mid = (mid[:, 0:256] + mid[:, 256:512]) + (mid[:, 512:768] + mid[:, 768:1024])
        mh, ml = split(mid)
        total = total + dot(lead1[...], mh) + dot(lead1[...], ml)
        up, down = x[0:128], x[128:256]
        weight = pltpu.roll(down, 127, 1)
        nu = up / jnp.maximum(jnp.where(ln % 32 == 20, weight, down), 1.0)
        nd = down / jnp.maximum(weight, 1.0)
        coarse = jnp.where(ln % 32 == 22, pltpu.roll(nd, 2, 1), nu)
        coarse = jnp.where((ln % 32 >= 20) & (ln % 32 < 23), coarse, 0.0)
        ch, cl = split(coarse)
        far = (dot(ch, spread2[...]) + dot(cl, spread2[...])) * wide2[...]
        far = (far[:, 0:256] + far[:, 256:512]) + (far[:, 512:768] + far[:, 768:1024])
        fh, fl = split(far)
        total = total + dot(lead2[0:64], fh) + dot(lead2[64:128], fh) + dot(lead2[0:64], fl)
        even, odd = total[0:32], total[32:64]
        pic[0] = jnp.where(low, even[:, 0:128], pltpu.roll(odd[:, 0:128], 64, 1))
        pic[1] = jnp.where(low, pltpu.roll(even[:, 0:128], 64, 1), odd[:, 0:128])
        pic[2] = jnp.where(low, even[:, 128:256], pltpu.roll(odd[:, 128:256], 64, 1))
        for m in range(32):
            for c in range(3):
                out_ref[t, c : c + 1, m * 128 : m * 128 + 128] = pic[c, m : m + 1, :]


def collapse(msg):
    vmem = pl.BlockSpec(memory_space=pltpu.VMEM)
    tables = [jnp.asarray(t) for t in collapse_tables()]
    return pl.pallas_call(
        collapse_kernel,
        out_shape=jax.ShapeDtypeStruct((4, 3, 4096), F32),
        in_specs=[vmem] * (1 + len(tables)),
        out_specs=vmem,
        scratch_shapes=[pltpu.VMEM((1024, 128), F32), pltpu.VMEM((3, 32, 128), F32)],
        compiler_params=pltpu.CompilerParams(vmem_limit_bytes=48 << 20),
        name="collapse",
    )(msg, *tables)


def local(frames, weight_map, seam_mask, strip_cell, partner, tile_group, tile_position_in_group):
    ids = tile_group[0, :, 0] * 16 + tile_position_in_group[0]
    g = jnp.arange(4, dtype=I32)
    column = strip_cell[0] + (g - strip_cell[0]) % 4
    hot = (jnp.arange(16, dtype=I32)[None, :] == (column // 4)[:, None]).astype(I32)
    strip_ids = jnp.sum(ids.reshape(2, 1, 16) * hot[None], axis=2).reshape(8)
    meta = jnp.concatenate([ids, strip_ids, partner, jnp.zeros((23,), I32)]).reshape(1, 64)
    metas = lax.all_gather(meta, AXES, axis=0, tiled=True)
    sent = encode(strip_cell, frames, weight_map, seam_mask)
    got = lax.all_to_all(sent, AXES, split_axis=0, concat_axis=0, tiled=True)
    main_ids = metas[:, :32].reshape(GROUPS, 4, 32).transpose(0, 2, 1).reshape(GROUPS, 128)
    side = metas[:, 32:41].T
    summed = merge(main_ids, side[:8], side[8:9], got)
    back = lax.all_to_all(summed.reshape(DEV, 4, 128), AXES, split_axis=0, concat_axis=0, tiled=True)
    return collapse(back.reshape(TILES, 128))


def solution(mesh):
    in_specs = (
        P(AXES, None, None, None),
        P(AXES, None, None),
        P(AXES, None, None),
        P(AXES),
        P(AXES),
        P(AXES, None, None),
        P(AXES, None),
    )
    return jax.shard_map(
        local, mesh=mesh, in_specs=in_specs, out_specs=P(AXES, None, None), check_vma=False
    )
```

time: 579 us -> 343 us (0.59); the launches traced: 569 us -> 343 us
  local copies, waits for them, and re-layouts: 268 us -> 12.1 us
  waiting for transfers between devices: 184 us -> 246 us
  other arithmetic: 60.4 us -> 1.12 us
  Pallas kernels: 0 us -> 30 us
  blocking collectives: 0 us -> 23.5 us
  matrix products: 18.1 us -> 0 us
    unnamed x3 -> x2, waiting for transfers between devices: 48.4 us -> 246 us
    slice x162 -> x3, local copies, waits for them, and re-layouts: 174 us -> 1.79 us  [the longest x1 1.79 us: local(): side = metas[:, 32:41].T]
    all_to_all x2 -> x1, waiting for transfers between devices: 125 us -> 0.01 us  [local(): got = lax.all_to_all(sent, AXES, split_axis=0, concat_axis=0, tiled=True)]
    pallas_call x0 -> x3, Pallas kernels: none -> 30 us  [the longest x1 19.9 us: merge(): pl.pallas_call(merge_kernel, out_shape=jax.ShapeDtypeStruct((TILES, 128),...]
    another operation x49 -> x0, other arithmetic: 29.1 us -> none
    reshape x70 -> x2, local copies, waits for them, and re-layouts: 29.3 us -> 0.98 us  [the longest x1 0.9 us: local(): metas[:, :32].reshape(GROUPS, 4, 32).transpose(0, 2, 1).reshape(GROUPS, 128)]
    all_to_all x0 -> x1, blocking collectives: none -> 23.5 us  [local(): lax.all_to_all(summed.reshape(DEV, 4, 128), AXES, split_axis=0, concat_ax...]
    dot_general x4 -> x0, matrix products: 18.1 us -> none  [the longest x1 7.92 us: local(): jnp.dot(select, piece, preferred_element_type=jnp.float32)]
  transfers between devices with their start and end apart: 4 -> 2, of which waited for: 3 -> 1; matrix products, arithmetic and copies ran while one was open for 49% -> 3% of each run, Pallas kernels for 0% -> 0%
where the time goes in v1:
time: 343 us
  waiting for transfers between devices  246 us (72%)
  Pallas kernels  30 us (9%)
  blocking collectives  23.5 us (7%)
  starting transfers between devices  15.7 us (5%)
  between operations  14.9 us (4%)
  local copies, waits for them, and re-layouts  12.1 us (4%)
    unnamed x2, waiting for transfers between devices  246 us
    all_to_all x1, blocking collectives, local(): lax.all_to_all(summed.reshape(DEV, 4, 128), AXES, split_axis=0, concat_ax...  23.5 us
    pallas_call x1, Pallas kernels, merge(): pl.pallas_call(merge_kernel, out_shape=jax.ShapeDtypeStruct((TILES, 128),...  19.9 us
    all_to_all x1, starting transfers between devices, local(): got = lax.all_to_all(sent, AXES, split_axis=0, concat_axis=0, tiled=True)  15.7 us
  transfers between devices with their start and end apart: 2, of which 1 were waited for; matrix products, arithmetic and copies ran while one was open for 3% of the time, Pallas kernels for 0%

profile of v1, /device:TPU:1, one launch (start us, length us, event | category | flops | bytes accessed | tf_op | source)
XLA Modules:
  0.0 342.8 jit_solution(15839399702827032126)
XLA Ops:
  7.2 0.8 copy.27.mask_ref
  8.0 0.0 copy-start.1
  8.1 1.1 copy-done.1
  9.2 0.0 copy-start.3
  9.2 0.9 copy-done.3
  10.1 6.5 %encode.1 = bf16[256,24,128]{2,1,0:T(8,128)(2,1)} custom-call(s32[1]{0:T(128)} %copy.33.cell_ref, bf16[1,3,128,1024]{3,2,1,0:T(8,128)(2,1)S(1)} %copy-done.1, bf16[1,128,1024]{2,1,0:T(8,128)(2,1)S(1)} %copy-done.3, s32[1,128,64]{2,1,0:T(8,128)S(1)} %copy.27.mask_ref), custom_call_target="tpu_custom_call" | custom-call | tf_op jit(solution)/shard_map/encode/pallas_call | solution.py:233
  16.6 0.0 copy-start.13
  16.6 0.0 copy-start.12
  16.6 15.7 %all-to-all-start = ((bf16[256,24,128]{2,1,0:T(8,128)(2,1)}), bf16[256,24,128]{2,1,0:T(8,128)(2,1)S(1)}, u32[]{:S(2)}, u32[]{:S(2)}) async-start(bf16[256,24,128]{2,1,0:T(8,128)(2,1)} %encode.1), calls=%async_computation | async-start | bytes 3145728 | tf_op jit(solution)/shard_map/all_to_all | solution.py:488
  32.3 0.0 all-reduce.3.cloned.1.call-start
  33.0 0.5 broadcast.98
  33.6 0.0 copy-done.13
  33.6 0.7 reduce.7
  34.2 0.1 squeeze.11
  34.3 0.0 copy-done.12
  34.3 0.1 mul.32
  34.4 0.1 fusion
  34.5 0.1 multiply_reduce_fusion
  34.6 0.1 reshape.84
  34.8 0.2 add_dynamic-update-slice_fusion
  35.0 0.0 copy-start.11
  35.0 0.6 copy-done.11
  35.6 0.0 all-reduce.3.cloned.1.call-update
  35.6 245.5 %all-reduce.3.cloned.1.call-done = s32[16384]{0:T(1024)} async-done(((s32[16384]{0:T(1024)}), s32[16384]{0:T(1024)}) %all-reduce.3.cloned.1.call-update) | async-done | bytes 65552
  281.1 1.6 reshape.90
  282.7 0.0 copy-start
  282.7 0.0 copy-start.2
  282.7 0.0 copy-start.4
  282.7 0.0 copy-start.9
  282.7 0.0 copy-start.10
  282.7 1.8 slice.17
  284.5 1.0 copy.30
  285.5 1.6 copy.25
  287.1 0.9 copy.28.ids_ref
  288.0 0.0 all-to-all-done.msg_ref
  288.0 0.0 copy-start.5
  288.0 0.0 copy-start.6
  288.0 0.0 copy-start.7
  288.1 0.0 copy-start.8
  288.1 19.9 %merge.1 = bf16[1024,128]{1,0:T(8,128)(2,1)S(1)} custom-call(s32[64,128]{1,0:T(8,128)S(1)} %copy.28.ids_ref, s32[8,256]{1,0:T(8,128)S(1)} %slice.18.sids_ref, s32[1,256]{1,0:T(1,128)S(1)} %slice.19.partner_ref, bf16[256,24,128]{2,1,0:T(8,128)(2,1)S(1)} %all-to-all-done.msg_ref), custom_call_target="tpu_custom_call" | custom-call | tf_op jit(solution)/shard_map/merge/pallas_call | solution.py:341
  308.0 23.5 %all_to_all.10 = bf16[256,4,128]{2,1,0:T(4,128)(2,1)S(1)} all-to-all(bf16[256,4,128]{2,1,0:T(4,128)(2,1)S(1)} %bitcast.15), channel_id=1, replica_groups=mesh['frames'=64,'tiles'=4] {'frames','tiles'}, dimensions={0} | all-to-all | bytes 524288 | tf_op jit(solution)/shard_map/all_to_all | solution.py:492
  331.5 0.0 copy-done
  331.5 0.0 copy-done.2
  331.5 0.0 copy-done.4
  331.5 0.0 copy-done.9
  331.5 0.0 copy-done.10
  331.5 0.0 copy-done.5
  331.5 0.0 copy-done.6
  331.5 0.0 copy-done.7
  331.5 0.0 copy-done.8
  331.5 3.6 %collapse.1 = f32[4,3,4096]{2,1,0:T(4,128)S(1)} custom-call(bf16[1024,128]{1,0:T(8,128)(2,1)S(1)} %bitcast.14, bf16[64,1024]{1,0:T(8,128)(2,1)S(1)} %copy-done.8, bf16[64,256]{1,0:T(8,128)(2,1)S(1)} %copy-done.10, bf16[128,128]{1,0:T(8,128)(2,1)S(1)} %copy-done.9, bf16[128,1024]{1,0:T(8,128)(2,1)S(1)} %copy-done.7, bf16[128,1024]{1,0:T(8,128)(2,1)S(1)} %copy-done.6, ...), custom_call_target="tpu_custom_call" | custom-call | tf_op jit(solution)/shard_map/collapse/pallas_call | solution.py:468
  335.2 0.8 copy.29
  (8 shorter events, 0.1 us)
Async XLA Ops:
  8.0 1.1 copy-start.1
  9.2 0.9 copy-start.3
  16.6 16.9 %copy-start.13 = (s32[1,32]{1,0:T(1,128)S(1)}, s32[1,32]{1,0:T(1,128)}, u32[]{:S(2)}) copy-start(s32[1,32]{1,0:T(1,128)} %param.22) | copy-start | bytes 388
  16.6 17.7 %copy-start.12 = (s32[1,32,1]{1,2,0:T(1,128)S(1)}, s32[1,32,1]{1,2,0:T(1,128)}, u32[]{:S(2)}) copy-start(s32[1,32,1]{1,2,0:T(1,128)} %param.21) | copy-start | bytes 388
  16.6 271.4 %all-to-all-start = ((bf16[256,24,128]{2,1,0:T(8,128)(2,1)}), bf16[256,24,128]{2,1,0:T(8,128)(2,1)S(1)}, u32[]{:S(2)}, u32[]{:S(2)}) async-start(bf16[256,24,128]{2,1,0:T(8,128)(2,1)} %encode.1), calls=%async_computation | async-start | bytes 3145728 | tf_op jit(solution)/shard_map/all_to_all | solution.py:488
  32.3 248.8 %all-reduce.3.cloned.1.call-start = ((), (), s32[]{:S(2)}) async-start(), calls=%async_computation.2 | async-start | bytes 131072
  35.0 0.6 copy-start.11
  282.7 48.8 %copy-start = (f32[256,1024]{1,0:T(8,128)S(1)}, f32[256,1024]{1,0:T(8,128)}, u32[]{:S(2)}) copy-start(f32[256,1024]{1,0:T(8,128)} %constant.57.clone.wide1) | copy-start | bytes 3145732
  282.7 48.8 %copy-start.2 = (f32[128,1024]{1,0:T(8,128)S(1)}, f32[128,1024]{1,0:T(8,128)}, u32[]{:S(2)}) copy-start(f32[128,1024]{1,0:T(8,128)} %constant.58.clone.wide2) | copy-start | bytes 1572868
  282.7 48.8 %copy-start.4 = (f32[256,256]{1,0:T(8,128)S(1)}, f32[256,256]{1,0:T(8,128)}, u32[]{:S(2)}) copy-start(f32[256,256]{1,0:T(8,128)} %constant.56.clone.keep0) | copy-start | bytes 786436
  282.7 48.8 %copy-start.9 = (bf16[128,128]{1,0:T(8,128)(2,1)S(1)}, bf16[128,128]{1,0:T(8,128)(2,1)}, u32[]{:S(2)}) copy-start(bf16[128,128]{1,0:T(8,128)(2,1)} %constant.52.clone.lead2) | copy-start | bytes 98308
  282.7 48.8 %copy-start.10 = (bf16[64,256]{1,0:T(8,128)(2,1)S(1)}, bf16[64,256]{1,0:T(8,128)(2,1)}, u32[]{:S(2)}) copy-start(bf16[64,256]{1,0:T(8,128)(2,1)} %constant.51.clone.lead1) | copy-start | bytes 98308
  288.0 43.5 %copy-start.5 = (bf16[128,1024]{1,0:T(8,128)(2,1)S(1)}, bf16[128,1024]{1,0:T(8,128)(2,1)}, u32[]{:S(2)}) copy-start(bf16[128,1024]{1,0:T(8,128)(2,1)} %constant.55.clone.spread2) | copy-start | bytes 786436
  288.0 43.5 %copy-start.6 = (bf16[128,1024]{1,0:T(8,128)(2,1)S(1)}, bf16[128,1024]{1,0:T(8,128)(2,1)}, u32[]{:S(2)}) copy-start(bf16[128,1024]{1,0:T(8,128)(2,1)} %constant.54.clone.spread1) | copy-start | bytes 786436
  288.0 43.5 %copy-start.7 = (bf16[128,1024]{1,0:T(8,128)(2,1)S(1)}, bf16[128,1024]{1,0:T(8,128)(2,1)}, u32[]{:S(2)}) copy-start(bf16[128,1024]{1,0:T(8,128)(2,1)} %constant.53.clone.spread0) | copy-start | bytes 786436
  288.1 43.5 %copy-start.8 = (bf16[64,1024]{1,0:T(8,128)(2,1)S(1)}, bf16[64,1024]{1,0:T(8,128)(2,1)}, u32[]{:S(2)}) copy-start(bf16[64,1024]{1,0:T(8,128)(2,1)} %constant.50.clone.lead0) | copy-start | bytes 393220
Sparse Core Ops, SparseCore 0:
  38.6 242.4 all-reduce.2

commit v2 on v1

--- a/solution.py
+++ b/solution.py
@@ -16,6 +16,7 @@
 ROWS = 24
 TILES = 1024
 GROUPS = 64
+DELTA_LANE, PARTNER_LANE, CELL_LANE = 114, 115, 118
 
 
 def iota(shape, axis):
@@ -34,7 +35,9 @@
     return (a + e) * (1.0 / 16.0) + (b + d) * 0.25 + c * 0.375
 
 
-def encode_kernel(cell_ref, frames_ref, weight_ref, mask_ref, out_ref, perm, zbuf, lev0, half, tail, *levs):
+def encode_kernel(
+    cell_ref, partner_ref, group_ref, position_ref, frames_ref, weight_ref, mask_ref, out_ref, perm, zbuf, lev0, half, tail, *levs
+):
     cell = cell_ref[0]
     sub = iota((8, 128), 0)
     lane = iota((8, 128), 1)
@@ -145,6 +148,17 @@
     kp, np_ = iota((128, 128), 0), iota((128, 128), 1)
     pick = (kp == (np_ // 4 % 2) * 64 + cell + np_ % 4).astype(F32).astype(BF16)
     slot = lane // 8
+    packed1 = lane // 4 * 2 + lane % 4 - 2
+    slot1 = jnp.where(lane % 4 >= 2, packed1 // 8, -1)
+    np1 = np_ // 4 * 2 + np_ % 4 - 2
+    pick1 = ((np_ % 4 >= 2) & (kp == (np1 // 4 % 2) * 64 + cell + np1 % 4)).astype(F32).astype(BF16)
+    kt, nt = iota((32, 128), 0), iota((32, 128), 1)
+    meta = jnp.zeros((8, 128), F32)
+    for e, ref in ((0, group_ref), (1, position_ref)):
+        spot = ((kt == nt // 4) & (nt % 4 == e)).astype(F32).astype(BF16)
+        meta = meta + dot(jnp.broadcast_to(ref[...], (8, 32)).astype(F32).astype(BF16), spot)
+    for at, value in ((DELTA_LANE, cell % 4), (PARTNER_LANE, partner_ref[0] // 4), (CELL_LANE, cell // 4)):
+        meta = jnp.where(lane == at, value.astype(F32), meta)
 
     tail[...] = jnp.zeros(tail.shape, F32)
 
@@ -153,7 +167,7 @@
         own = w * jnp.where(strip, m, 1.0)
         q = w * (1.0 - m)
         data = [own * b for b in bands] + [w]
-        picked = dot(jnp.concatenate([bands[0], bands[1], bands[2], q], axis=0).astype(BF16), pick)
+        picked = dot(jnp.concatenate([bands[0], bands[1], bands[2], q], axis=0).astype(BF16), pick if k == 0 else pick1)
         return data, [picked[8 * i : 8 * i + 8] for i in range(4)]
 
     for k in range(4, -1, -1):
@@ -207,10 +221,9 @@
                     base = (r * 8 + a) * 64
                     for i in range(4):
                         tail[pl.ds(base + i, 8, stride=8), :] = data[i]
-                    u = jnp.zeros((8, 128), F32)
+                    u = meta
                     for i in range(4):
-                        u = jnp.where(slot == i, picked[i], u)
-                    u = jnp.where(low, u, (cell % 4).astype(F32))
+                        u = jnp.where(slot1 == i, picked[i], u)
                     old = tail[pl.ds(base + 7, 8, stride=8), :]
                     tail[pl.ds(base + 7, 8, stride=8), :] = old + u
                 else:
@@ -219,21 +232,21 @@
                         base = (p * 128 + c * 8) * 8
                         for e in range(2):
                             tail[pl.ds(base + 4 + e, 8, stride=8), :] = data[2 * p + e]
-                        u = jnp.where(slot == 4, picked[2 * p], 0.0)
+                        u = jnp.where(slot1 == 4, picked[2 * p], 0.0)
                         if p == 0:
-                            u = jnp.where(slot == 5, picked[1], u)
-                        u = jnp.where(slot == 6, picked[3], u)
+                            u = jnp.where(slot1 == 5, picked[1], u)
+                        u = jnp.where(slot1 == 6, picked[3], u)
                         tail[pl.ds(base + 7, 8, stride=8), :] = u
     for d in range(DEV):
         out_ref[d, 16:24, :] = tail[d * 8 : d * 8 + 8, :].astype(BF16)
 
 
-def encode(cell, frames, weight, mask):
+def encode(cell, partner, group, position, frames, weight, mask):
     vmem = pl.BlockSpec(memory_space=pltpu.VMEM)
     return pl.pallas_call(
         encode_kernel,
         out_shape=jax.ShapeDtypeStruct((DEV, ROWS, 128), BF16),
-        in_specs=[pl.BlockSpec(memory_space=pltpu.SMEM), vmem, vmem, vmem],
+        in_specs=[pl.BlockSpec(memory_space=pltpu.SMEM)] * 2 + [vmem] * 5,
         out_specs=vmem,
         scratch_shapes=[
             pltpu.VMEM((1024, 1024), BF16),
@@ -245,10 +258,10 @@
         + [pltpu.VMEM((5, max(8 >> k, 1), 16 >> k, 8, 128), F32) for k in range(1, 5)],
         compiler_params=pltpu.CompilerParams(vmem_limit_bytes=48 << 20),
         name="encode",
-    )(cell, frames, weight, mask)
-
-
-def merge_kernel(ids_ref, sids_ref, partner_ref, msg_ref, out_ref, table, tail, acc):
+    )(cell, partner, group, position, frames, weight, mask)
+
+
+def merge_kernel(msg_ref, out_ref, table, tail, ids, acc):
     lane = iota((8, 128), 1)
     bit1, bit0 = lane // 2 % 2 == 0, lane % 2 == 0
     zero8 = jnp.zeros((8, 128), F32)
@@ -259,8 +272,7 @@
             jnp.where(keep, pltpu.roll(a, 128 - by, 1), b),
         )
 
-    @pl.loop(0, GROUPS)
-    def _(j):
+    def arrange(j):
         x = [msg_ref[4 * j + s].astype(F32) for s in range(4)]
         for s in range(4):
             tail[4 * j + s] = x[s][16:24]
@@ -275,13 +287,38 @@
                 parts[g].append(v[g])
         for g in range(4):
             table[j, g * 32 : g * 32 + 32, :] = jnp.concatenate(parts[g] + [zero8], axis=0).astype(BF16)
-
-    fr = iota((DEV, DEV), 0)
-    swap_rows = (fr == partner_ref[...]).astype(F32).astype(BF16)
+        ids[pl.ds(j, 1), :] = (parts[0][2][7:8] * 16.0 + parts[1][2][7:8]).astype(I32)
+
+    @pl.loop(0, GROUPS // 4)
+    def _(j):
+        for s in range(4):
+            arrange(4 * j + s)
+
     p0 = tail[:, 6, :]
     p1 = tail[:, 7, :]
+    p0b, p1b = p0.astype(BF16), p1.astype(BF16)
+    kl, nl = iota((128, 256), 0), iota((128, 256), 1)
     ln = iota((DEV, 128), 1)
-    s0 = dot(swap_rows, p0.astype(BF16))
+
+    def spread(at):
+        return dot(p1b, (kl == at).astype(F32).astype(BF16))
+
+    wanted = spread(PARTNER_LANE).astype(I32) * 4 + iota((DEV, DEV), 0) % 4
+    swap_rows = (wanted == iota((DEV, DEV), 1)).astype(F32).astype(BF16)
+    shift = spread(DELTA_LANE)[:, :128]
+    cell = spread(CELL_LANE)[:, :128].astype(I32)
+    ks, ns = iota((8, 128), 0), iota((8, 128), 1)
+    chosen = (((ks < 4) & (ns // 64 == ks // 2) & (ns % 4 == ks % 2)) | ((ks >= 4) & (ns == DELTA_LANE)))
+    chosen = chosen.astype(F32).astype(BF16)
+    under = []
+    for e in range(2):
+        here = (ln // 4 % 16 == cell + e) & (ln % 4 < 2) | (ln == DELTA_LANE)
+        found = dot_t(chosen, jnp.where(here, p1, 0.0).astype(BF16))
+        under.append([(found[2 * b : 2 * b + 1] * 16.0 + found[2 * b + 1 : 2 * b + 2]).astype(I32) for b in range(2)])
+        delta_row = found[4:5]
+    pack = ((kl % 4 >= 2) & (kl // 4 * 2 + kl % 4 - 2 == nl))[:, :128].astype(F32).astype(BF16)
+    p1 = dot(p1b, pack)
+    s0 = dot(swap_rows, p0b)
     s1 = dot(swap_rows, p1.astype(BF16))
     q0 = jnp.where(
         ln < 32,
@@ -298,7 +335,6 @@
             jnp.where((sl == 2) | (sl == 5), pltpu.roll(p1, 120, 1), 0.0),
         ),
     )
-    shift = jnp.where(ln < 64, pltpu.roll(p1, 64, 1), p1)
 
     def turn(c):
         result = c
@@ -315,14 +351,15 @@
     tile = iota((TILES, 256), 0)
     acc[...] = jnp.zeros((TILES, 128), F32)
     for s in range(8):
-        hot = (tile == sids_ref[s : s + 1, :]).astype(F32).astype(BF16)
+        strip_ids = jnp.where(delta_row > float(s % 4), under[1][s // 4], under[0][s // 4])
+        hot = (tile == strip_ids).astype(F32).astype(BF16)
         acc[...] += dot(hot, extra[:, s * 128 : s * 128 + 128])
 
     @pl.loop(0, GROUPS // 4)
     def _(j):
         hots, datas = [], []
         for s in range(4):
-            row = ids_ref[pl.ds(4 * j + s, 1), :]
+            row = ids[pl.ds(4 * j + s, 1), :]
             hots.append((iota((TILES, 128), 0) == row).astype(F32).astype(BF16))
             datas.append(table[4 * j + s])
         acc[...] += dot_t(jnp.concatenate(hots, axis=1), jnp.concatenate(datas, axis=1))
@@ -336,21 +373,22 @@
     out_ref[...] = (sums / jnp.maximum(den, 1.0)).astype(BF16)
 
 
-def merge(ids, sids, partner, msg):
+def merge(msg):
     vmem = pl.BlockSpec(memory_space=pltpu.VMEM)
     return pl.pallas_call(
         merge_kernel,
         out_shape=jax.ShapeDtypeStruct((TILES, 128), BF16),
-        in_specs=[vmem] * 4,
+        in_specs=[vmem],
         out_specs=vmem,
         scratch_shapes=[
             pltpu.VMEM((GROUPS, 128, 128), BF16),
             pltpu.VMEM((DEV, 8, 128), F32),
+            pltpu.VMEM((GROUPS, 128), I32),
             pltpu.VMEM((TILES, 128), F32),
         ],
         compiler_params=pltpu.CompilerParams(vmem_limit_bytes=48 << 20),
         name="merge",
-    )(ids, sids, partner, msg)
+    )(msg)
 
 
 def grow_matrices():
@@ -477,18 +515,11 @@
 
 
 def local(frames, weight_map, seam_mask, strip_cell, partner, tile_group, tile_position_in_group):
-    ids = tile_group[0, :, 0] * 16 + tile_position_in_group[0]
-    g = jnp.arange(4, dtype=I32)
-    column = strip_cell[0] + (g - strip_cell[0]) % 4
-    hot = (jnp.arange(16, dtype=I32)[None, :] == (column // 4)[:, None]).astype(I32)
-    strip_ids = jnp.sum(ids.reshape(2, 1, 16) * hot[None], axis=2).reshape(8)
-    meta = jnp.concatenate([ids, strip_ids, partner, jnp.zeros((23,), I32)]).reshape(1, 64)
-    metas = lax.all_gather(meta, AXES, axis=0, tiled=True)
-    sent = encode(strip_cell, frames, weight_map, seam_mask)
+    sent = encode(
+        strip_cell, partner, tile_group.reshape(1, 32), tile_position_in_group, frames, weight_map, seam_mask
+    )
     got = lax.all_to_all(sent, AXES, split_axis=0, concat_axis=0, tiled=True)
-    main_ids = metas[:, :32].reshape(GROUPS, 4, 32).transpose(0, 2, 1).reshape(GROUPS, 128)
-    side = metas[:, 32:41].T
-    summed = merge(main_ids, side[:8], side[8:9], got)
+    summed = merge(got)
     back = lax.all_to_all(summed.reshape(DEV, 4, 128), AXES, split_axis=0, concat_axis=0, tiled=True)
     return collapse(back.reshape(TILES, 128))
 

time: 343 us -> 110 us (0.32)
  waiting for transfers between devices: 246 us -> 0 us
  blocking collectives: 23.5 us -> 80.6 us
  starting transfers between devices: 15.7 us -> 0 us
  between operations: 14.9 us -> 1.43 us
  Pallas kernels: 30 us -> 22.2 us
  local copies, waits for them, and re-layouts: 12.1 us -> 5.09 us
    unnamed x2 -> x0, waiting for transfers between devices: 246 us -> none
    all_to_all x0 -> x1, blocking collectives: none -> 59.2 us  [local(): got = lax.all_to_all(sent, AXES, split_axis=0, concat_axis=0, tiled=True)]
    all_to_all x1 -> x0, starting transfers between devices: 15.7 us -> none  [local(): got = lax.all_to_all(sent, AXES, split_axis=0, concat_axis=0, tiled=True)]
    pallas_call x1, Pallas kernels: 19.9 us -> 13.2 us  [merge(): pl.pallas_call(merge_kernel, out_shape=jax.ShapeDtypeStruct((TILES, 128),...]
  transfers between devices with their start and end apart: 2 -> 0, of which waited for: 1 -> 0; matrix products, arithmetic and copies ran while one was open for 3% -> 0% of each run, Pallas kernels for 0% -> 0%
where the time goes in v2:
time: 110 us; the launch traced here: 109 us
  blocking collectives  80.6 us (73%)
  Pallas kernels  22.2 us (20%)
  local copies, waits for them, and re-layouts  5.09 us (5%)
  between operations  1.43 us (1%)
    all_to_all x1, blocking collectives, local(): got = lax.all_to_all(sent, AXES, split_axis=0, concat_axis=0, tiled=True)  59.2 us
    all_to_all x1, blocking collectives, local(): lax.all_to_all(summed.reshape(DEV, 4, 128), AXES, split_axis=0, concat_ax...  21.4 us
    pallas_call x1, Pallas kernels, merge(): pl.pallas_call(merge_kernel, out_shape=jax.ShapeDtypeStruct((TILES, 128),...  13.2 us
    pallas_call x1, Pallas kernels, encode(): pl.pallas_call(encode_kernel, out_shape=jax.ShapeDtypeStruct((DEV, ROWS,...  5.34 us
    unnamed x27, local copies, waits for them, and re-layouts  4.29 us
    pallas_call x1, Pallas kernels, collapse(): pl.pallas_call(collapse_kernel, out_shape=jax.ShapeDtypeStruct((4, 3, 409...  3.7 us

profile of v2, /device:TPU:1, one launch (start us, length us, event | category | flops | bytes accessed | tf_op | source)
XLA Modules:
  0.0 109.4 jit_solution(8517402802487052105)
XLA Ops:
  1.3 0.8 copy.17.mask_ref
  2.2 0.0 copy-start.1
  2.2 1.1 %copy-done.1 = bf16[1,3,128,1024]{3,2,1,0:T(8,128)(2,1)S(1)} copy-done((bf16[1,3,128,1024]{3,2,1,0:T(8,128)(2,1)S(1)}, bf16[1,3,128,1024]{3,2,1,0:T(8,128)(2,1)}, u32[]{:S(2)}) %copy-start.1) | copy-done | bytes 786456
  3.3 0.0 copy-start.3
  3.3 0.9 copy-done.3
  4.2 0.0 copy-start.11
  4.2 0.7 copy-done.11
  4.9 0.0 copy-start.12
  4.9 0.7 copy-done.12
  5.6 5.3 %encode.1 = bf16[256,24,128]{2,1,0:T(8,128)(2,1)S(1)} custom-call(s32[1]{0:T(128)S(6)} %copy.19.cell_ref, s32[1]{0:T(128)S(6)} %copy.20.partner_ref, s32[1,32]{1,0:T(1,128)S(1)} %bitcast.5, s32[1,32]{1,0:T(1,128)S(1)} %copy-done.12, bf16[1,3,128,1024]{3,2,1,0:T(8,128)(2,1)S(1)} %copy-done.1, bf16[1,128,1024]{2,1,0:T(8,128)(2,1)S(1)} %copy-done.3, ...), custom_call_target="tpu_custom_call" | custom-call | tf_op jit(solution)/shard_map/encode/pallas_call | solution.py:246
  10.9 0.0 copy-start.7
  10.9 0.0 copy-start.8
  10.9 0.0 copy-start.9
  10.9 0.0 copy-start.10
  10.9 59.2 %all_to_all.10.msg_ref = bf16[256,24,128]{2,1,0:T(8,128)(2,1)S(1)} all-to-all(bf16[256,24,128]{2,1,0:T(8,128)(2,1)S(1)} %encode.1), channel_id=1, replica_groups=mesh['frames'=64,'tiles'=4] {'frames','tiles'}, dimensions={0} | all-to-all | bytes 3145728 | tf_op jit(solution)/shard_map/all_to_all | solution.py:521
  70.2 0.0 copy-start
  70.2 0.0 copy-start.2
  70.2 0.0 copy-start.4
  70.2 0.0 copy-start.5
  70.2 0.0 copy-start.6
  70.2 13.2 %merge.1 = bf16[1024,128]{1,0:T(8,128)(2,1)S(1)} custom-call(bf16[256,24,128]{2,1,0:T(8,128)(2,1)S(1)} %all_to_all.10.msg_ref), custom_call_target="tpu_custom_call" | custom-call | tf_op jit(solution)/shard_map/merge/pallas_call | solution.py:378
  83.4 21.4 %all_to_all.11 = bf16[256,4,128]{2,1,0:T(4,128)(2,1)S(1)} all-to-all(bf16[256,4,128]{2,1,0:T(4,128)(2,1)S(1)} %bitcast.4), channel_id=1, replica_groups=mesh['frames'=64,'tiles'=4] {'frames','tiles'}, dimensions={0} | all-to-all | bytes 524288 | tf_op jit(solution)/shard_map/all_to_all | solution.py:523
  104.8 0.0 copy-done.7
  104.8 0.0 copy-done.8
  104.8 0.0 copy-done.9
  104.8 0.0 copy-done.10
  104.8 0.0 copy-done
  104.9 0.0 copy-done.2
  104.9 0.0 copy-done.4
  104.9 0.0 copy-done.5
  104.9 0.0 copy-done.6
  104.9 3.7 %collapse.1 = f32[4,3,4096]{2,1,0:T(4,128)S(1)} custom-call(bf16[1024,128]{1,0:T(8,128)(2,1)S(1)} %bitcast.3, bf16[64,1024]{1,0:T(8,128)(2,1)S(1)} %copy-done.8, bf16[64,256]{1,0:T(8,128)(2,1)S(1)} %copy-done.10, bf16[128,128]{1,0:T(8,128)(2,1)S(1)} %copy-done.9, bf16[128,1024]{1,0:T(8,128)(2,1)S(1)} %copy-done.7, bf16[128,1024]{1,0:T(8,128)(2,1)S(1)} %copy-done.6, ...), custom_call_target="tpu_custom_call" | custom-call | tf_op jit(solution)/shard_map/collapse/pallas_call | solution.py:506
  108.6 0.8 copy.18
Async XLA Ops:
  2.2 1.1 %copy-start.1 = (bf16[1,3,128,1024]{3,2,1,0:T(8,128)(2,1)S(1)}, bf16[1,3,128,1024]{3,2,1,0:T(8,128)(2,1)}, u32[]{:S(2)}) copy-start(bf16[1,3,128,1024]{3,2,1,0:T(8,128)(2,1)} %frames_ref.1) | copy-start | bytes 2359300
  3.3 0.9 copy-start.3
  4.2 0.7 copy-start.11
  4.9 0.7 copy-start.12
  10.9 93.9 %copy-start.7 = (bf16[128,1024]{1,0:T(8,128)(2,1)S(1)}, bf16[128,1024]{1,0:T(8,128)(2,1)}, u32[]{:S(2)}) copy-start(bf16[128,1024]{1,0:T(8,128)(2,1)} %constant.21.clone.spread0) | copy-start | bytes 786436
  10.9 93.9 %copy-start.8 = (bf16[64,1024]{1,0:T(8,128)(2,1)S(1)}, bf16[64,1024]{1,0:T(8,128)(2,1)}, u32[]{:S(2)}) copy-start(bf16[64,1024]{1,0:T(8,128)(2,1)} %constant.18.clone.lead0) | copy-start | bytes 393220
  10.9 93.9 %copy-start.9 = (bf16[128,128]{1,0:T(8,128)(2,1)S(1)}, bf16[128,128]{1,0:T(8,128)(2,1)}, u32[]{:S(2)}) copy-start(bf16[128,128]{1,0:T(8,128)(2,1)} %constant.20.clone.lead2) | copy-start | bytes 98308
  10.9 93.9 %copy-start.10 = (bf16[64,256]{1,0:T(8,128)(2,1)S(1)}, bf16[64,256]{1,0:T(8,128)(2,1)}, u32[]{:S(2)}) copy-start(bf16[64,256]{1,0:T(8,128)(2,1)} %constant.19.clone.lead1) | copy-start | bytes 98308
  70.2 34.7 %copy-start = (f32[256,1024]{1,0:T(8,128)S(1)}, f32[256,1024]{1,0:T(8,128)}, u32[]{:S(2)}) copy-start(f32[256,1024]{1,0:T(8,128)} %constant.25.clone.wide1) | copy-start | bytes 3145732
  70.2 34.7 %copy-start.2 = (f32[128,1024]{1,0:T(8,128)S(1)}, f32[128,1024]{1,0:T(8,128)}, u32[]{:S(2)}) copy-start(f32[128,1024]{1,0:T(8,128)} %constant.26.clone.wide2) | copy-start | bytes 1572868
  70.2 34.7 %copy-start.4 = (f32[256,256]{1,0:T(8,128)S(1)}, f32[256,256]{1,0:T(8,128)}, u32[]{:S(2)}) copy-start(f32[256,256]{1,0:T(8,128)} %constant.24.clone.keep0) | copy-start | bytes 786436
  70.2 34.7 %copy-start.5 = (bf16[128,1024]{1,0:T(8,128)(2,1)S(1)}, bf16[128,1024]{1,0:T(8,128)(2,1)}, u32[]{:S(2)}) copy-start(bf16[128,1024]{1,0:T(8,128)(2,1)} %constant.23.clone.spread2) | copy-start | bytes 786436
  70.2 34.7 %copy-start.6 = (bf16[128,1024]{1,0:T(8,128)(2,1)S(1)}, bf16[128,1024]{1,0:T(8,128)(2,1)}, u32[]{:S(2)}) copy-start(bf16[128,1024]{1,0:T(8,128)(2,1)} %constant.22.clone.spread1) | copy-start | bytes 786436

commit v3 on v2

--- a/solution.py
+++ b/solution.py
@@ -154,9 +154,10 @@
     pick1 = ((np_ % 4 >= 2) & (kp == (np1 // 4 % 2) * 64 + cell + np1 % 4)).astype(F32).astype(BF16)
     kt, nt = iota((32, 128), 0), iota((32, 128), 1)
     meta = jnp.zeros((8, 128), F32)
-    for e, ref in ((0, group_ref), (1, position_ref)):
+    group, position = group_ref[...], position_ref[...]
+    for e, part in ((0, position % 4 * 16 + group // 4), (1, group % 4 * 4 + position // 4)):
         spot = ((kt == nt // 4) & (nt % 4 == e)).astype(F32).astype(BF16)
-        meta = meta + dot(jnp.broadcast_to(ref[...], (8, 32)).astype(F32).astype(BF16), spot)
+        meta = meta + dot(jnp.broadcast_to(part, (8, 32)).astype(F32).astype(BF16), spot)
     for at, value in ((DELTA_LANE, cell % 4), (PARTNER_LANE, partner_ref[0] // 4), (CELL_LANE, cell // 4)):
         meta = jnp.where(lane == at, value.astype(F32), meta)
 
@@ -261,7 +262,46 @@
     )(cell, partner, group, position, frames, weight, mask)
 
 
-def merge_kernel(msg_ref, out_ref, table, tail, ids, acc):
+def one_hot(high, low):
+    n = high.shape[1]
+    here = (jnp.broadcast_to(low, (16, n)).astype(I32) == iota((16, n), 0)).astype(F32).astype(BF16)
+    high = jnp.broadcast_to(high, (16, n)).astype(BF16)
+    zero = jnp.zeros((16, n), BF16)
+    return jnp.concatenate([jnp.where(high == jnp.full((16, n), t, BF16), here, zero) for t in range(GROUPS)], axis=0)
+
+
+def place_of(p):
+    return (p // 4, p % 4)
+
+
+def merge_kernel(
+    msg_ref, out_ref, got, table, tail, ids, acc, wide, sums, send1, recv1, own1, send2, recv2, own2
+):
+    me = lax.axis_index("frames") * 4 + lax.axis_index("tiles")
+    barrier = pltpu.get_barrier_semaphore()
+
+    @pl.loop(1, DEV)
+    def _(i):
+        pl.semaphore_signal(
+            barrier, inc=1, device_id=place_of((me + i) % DEV), device_id_type=pl.DeviceIdType.MESH
+        )
+
+    pl.semaphore_wait(barrier, DEV - 1)
+    keep1 = pltpu.make_async_copy(msg_ref.at[me], got.at[me], own1)
+    keep1.start()
+
+    @pl.loop(1, DEV)
+    def _(i):
+        peer = (me + i) % DEV
+        pltpu.make_async_remote_copy(
+            src_ref=msg_ref.at[peer],
+            dst_ref=got.at[me],
+            send_sem=send1,
+            recv_sem=recv1.at[me // 16],
+            device_id=place_of(peer),
+            device_id_type=pl.DeviceIdType.MESH,
+        ).start()
+
     lane = iota((8, 128), 1)
     bit1, bit0 = lane // 2 % 2 == 0, lane % 2 == 0
     zero8 = jnp.zeros((8, 128), F32)
@@ -273,7 +313,7 @@
         )
 
     def arrange(j):
-        x = [msg_ref[4 * j + s].astype(F32) for s in range(4)]
+        x = [got[4 * j + s].astype(F32) for s in range(4)]
         for s in range(4):
             tail[4 * j + s] = x[s][16:24]
         parts = [[], [], [], []]
@@ -287,12 +327,31 @@
                 parts[g].append(v[g])
         for g in range(4):
             table[j, g * 32 : g * 32 + 32, :] = jnp.concatenate(parts[g] + [zero8], axis=0).astype(BF16)
-        ids[pl.ds(j, 1), :] = (parts[0][2][7:8] * 16.0 + parts[1][2][7:8]).astype(I32)
-
-    @pl.loop(0, GROUPS // 4)
-    def _(j):
+        ids[0, pl.ds(j, 1), :] = parts[0][2][7:8]
+        ids[1, pl.ds(j, 1), :] = parts[1][2][7:8]
+
+    acc[...] = jnp.zeros((TILES, 128), F32)
+
+    def add_block(j):
         for s in range(4):
             arrange(4 * j + s)
+        hots, datas = [], []
+        for s in range(4):
+            hots.append(one_hot(ids[0, pl.ds(4 * j + s, 1), :], ids[1, pl.ds(4 * j + s, 1), :]))
+            datas.append(table[4 * j + s])
+        acc[...] += dot_t(jnp.concatenate(hots, axis=1), jnp.concatenate(datas, axis=1))
+
+    @pl.loop(1, 16)
+    def _(k):
+        j = (me // 16 + 16 - k) % 16
+        some = got.at[pl.ds(0, 16)]
+        pltpu.make_async_copy(some, some, recv1.at[j]).wait()
+        add_block(j)
+
+    keep1.wait()
+    some = got.at[pl.ds(0, 15)]
+    pltpu.make_async_copy(some, some, recv1.at[me // 16]).wait()
+    add_block(me // 16)
 
     p0 = tail[:, 6, :]
     p1 = tail[:, 7, :]
@@ -314,7 +373,7 @@
     for e in range(2):
         here = (ln // 4 % 16 == cell + e) & (ln % 4 < 2) | (ln == DELTA_LANE)
         found = dot_t(chosen, jnp.where(here, p1, 0.0).astype(BF16))
-        under.append([(found[2 * b : 2 * b + 1] * 16.0 + found[2 * b + 1 : 2 * b + 2]).astype(I32) for b in range(2)])
+        under.append([(found[2 * b : 2 * b + 1], found[2 * b + 1 : 2 * b + 2]) for b in range(2)])
         delta_row = found[4:5]
     pack = ((kl % 4 >= 2) & (kl // 4 * 2 + kl % 4 - 2 == nl))[:, :128].astype(F32).astype(BF16)
     p1 = dot(p1b, pack)
@@ -348,45 +407,66 @@
     target = jnp.where(nq // 32 % 4 == nq // 128 % 4, (nq % 32) * 8 + nq // 128, -1)
     extra = dot(both, (kq == target).astype(F32).astype(BF16)).astype(BF16)
 
-    tile = iota((TILES, 256), 0)
-    acc[...] = jnp.zeros((TILES, 128), F32)
     for s in range(8):
-        strip_ids = jnp.where(delta_row > float(s % 4), under[1][s // 4], under[0][s // 4])
-        hot = (tile == strip_ids).astype(F32).astype(BF16)
+        next_block = delta_row > float(s % 4)
+        hot = one_hot(*(jnp.where(next_block, v, u) for u, v in zip(under[0][s // 4], under[1][s // 4])))
         acc[...] += dot(hot, extra[:, s * 128 : s * 128 + 128])
 
-    @pl.loop(0, GROUPS // 4)
-    def _(j):
-        hots, datas = [], []
-        for s in range(4):
-            row = ids[pl.ds(4 * j + s, 1), :]
-            hots.append((iota((TILES, 128), 0) == row).astype(F32).astype(BF16))
-            datas.append(table[4 * j + s])
-        acc[...] += dot_t(jnp.concatenate(hots, axis=1), jnp.concatenate(datas, axis=1))
-
-    sums = acc[...]
-    ln = iota((TILES, 128), 1)
+    ln = iota((DEV, 128), 1)
     r = ln % 32
-    den = jnp.ones((TILES, 128), F32)
-    for low, high, by in ((0, 4, 12), (4, 8, 8), (8, 12, 4), (16, 17, 3), (17, 18, 2), (18, 19, 1)):
-        den = jnp.where((r >= low) & (r < high), pltpu.roll(sums, 128 - by, 1), den)
-    out_ref[...] = (sums / jnp.maximum(den, 1.0)).astype(BF16)
+    for t in range(4):
+        total = acc[t * DEV : t * DEV + DEV, :]
+        den = jnp.ones((DEV, 128), F32)
+        for low, high, by in ((0, 4, 12), (4, 8, 8), (8, 12, 4), (16, 17, 3), (17, 18, 2), (18, 19, 1)):
+            den = jnp.where((r >= low) & (r < high), pltpu.roll(total, 128 - by, 1), den)
+        wide[:, t, :] = total / jnp.maximum(den, 1.0)
+    sums[...] = wide[...].astype(BF16)
+
+    keep2 = pltpu.make_async_copy(sums.at[me], out_ref.at[me], own2)
+    keep2.start()
+
+    @pl.loop(1, DEV)
+    def _(i):
+        peer = (me + i) % DEV
+        pltpu.make_async_remote_copy(
+            src_ref=sums.at[peer],
+            dst_ref=out_ref.at[me],
+            send_sem=send2,
+            recv_sem=recv2,
+            device_id=place_of(peer),
+            device_id_type=pl.DeviceIdType.MESH,
+        ).start()
+
+    keep2.wait()
+    for ref, sem in ((msg_ref, send1), (sums, send2), (out_ref, recv2)):
+        some = ref.at[pl.ds(0, DEV - 1)]
+        pltpu.make_async_copy(some, some, sem).wait()
 
 
 def merge(msg):
     vmem = pl.BlockSpec(memory_space=pltpu.VMEM)
+    one = pltpu.SemaphoreType.DMA
     return pl.pallas_call(
         merge_kernel,
-        out_shape=jax.ShapeDtypeStruct((TILES, 128), BF16),
+        out_shape=jax.ShapeDtypeStruct((DEV, 4, 128), BF16),
         in_specs=[vmem],
         out_specs=vmem,
         scratch_shapes=[
+            pltpu.VMEM((DEV, ROWS, 128), BF16),
             pltpu.VMEM((GROUPS, 128, 128), BF16),
             pltpu.VMEM((DEV, 8, 128), F32),
-            pltpu.VMEM((GROUPS, 128), I32),
+            pltpu.VMEM((2, GROUPS, 128), F32),
             pltpu.VMEM((TILES, 128), F32),
+            pltpu.VMEM((DEV, 4, 128), F32),
+            pltpu.VMEM((DEV, 4, 128), BF16),
+            one,
+            pltpu.SemaphoreType.DMA((16,)),
+            one,
+            one,
+            one,
+            one,
         ],
-        compiler_params=pltpu.CompilerParams(vmem_limit_bytes=48 << 20),
+        compiler_params=pltpu.CompilerParams(collective_id=1, has_side_effects=True, vmem_limit_bytes=48 << 20),
         name="merge",
     )(msg)
 
@@ -518,9 +598,7 @@
     sent = encode(
         strip_cell, partner, tile_group.reshape(1, 32), tile_position_in_group, frames, weight_map, seam_mask
     )
-    got = lax.all_to_all(sent, AXES, split_axis=0, concat_axis=0, tiled=True)
-    summed = merge(got)
-    back = lax.all_to_all(summed.reshape(DEV, 4, 128), AXES, split_axis=0, concat_axis=0, tiled=True)
+    back = merge(sent)
     return collapse(back.reshape(TILES, 128))
 
 

time: 110 us -> 86.7 us (0.79)
  blocking collectives: 80.6 us -> 0 us
  Pallas kernels: 22.2 us -> 79.9 us
    all_to_all x2 -> x0, blocking collectives: 80.6 us -> none  [the longest x1 59.2 us: local(): got = lax.all_to_all(sent, AXES, split_axis=0, concat_axis=0, tiled=True)]
    pallas_call x1, Pallas kernels: 13.2 us -> 71 us  [merge(): pl.pallas_call(merge_kernel, out_shape=jax.ShapeDtypeStruct((DEV, 4, 128)...]
where the time goes in v3:
time: 86.7 us; the launch traced here: 86.5 us
  Pallas kernels  79.9 us (92%)
  local copies, waits for them, and re-layouts  5.09 us (6%)
  between operations  1.45 us (2%)
    pallas_call x1, Pallas kernels, merge(): pl.pallas_call(merge_kernel, out_shape=jax.ShapeDtypeStruct((DEV, 4, 128)...  71 us
    pallas_call x1, Pallas kernels, encode(): pl.pallas_call(encode_kernel, out_shape=jax.ShapeDtypeStruct((DEV, ROWS,...  5.35 us
    unnamed x27, local copies, waits for them, and re-layouts  4.29 us
    pallas_call x1, Pallas kernels, collapse(): pl.pallas_call(collapse_kernel, out_shape=jax.ShapeDtypeStruct((4, 3, 409...  3.61 us

profile of v3, /device:TPU:1, one launch (start us, length us, event | category | flops | bytes accessed | tf_op | source)
XLA Modules:
  0.0 86.5 jit_solution(16508493008707697887)
XLA Ops:
  1.3 0.8 copy.17.mask_ref
  2.2 0.0 copy-start.1
  2.2 1.1 %copy-done.1 = bf16[1,3,128,1024]{3,2,1,0:T(8,128)(2,1)S(1)} copy-done((bf16[1,3,128,1024]{3,2,1,0:T(8,128)(2,1)S(1)}, bf16[1,3,128,1024]{3,2,1,0:T(8,128)(2,1)}, u32[]{:S(2)}) %copy-start.1) | copy-done | bytes 786456
  3.3 0.0 copy-start.3
  3.3 0.9 %copy-done.3 = bf16[1,128,1024]{2,1,0:T(8,128)(2,1)S(1)} copy-done((bf16[1,128,1024]{2,1,0:T(8,128)(2,1)S(1)}, bf16[1,128,1024]{2,1,0:T(8,128)(2,1)}, u32[]{:S(2)}) %copy-start.3) | copy-done | bytes 262168
  4.2 0.0 copy-start.11
  4.2 0.7 copy-done.11
  4.9 0.0 copy-start.12
  4.9 0.7 copy-done.12
  5.6 0.0 copy-start.5
  5.6 0.0 copy-start.6
  5.6 0.0 copy-start.7
  5.6 0.0 copy-start.8
  5.6 0.0 copy-start.9
  5.6 0.0 copy-start.10
  5.6 5.4 %encode.1.msg_ref = bf16[256,24,128]{2,1,0:T(8,128)(2,1)S(1)} custom-call(s32[1]{0:T(128)S(6)} %copy.19.cell_ref, s32[1]{0:T(128)S(6)} %copy.20.partner_ref, s32[1,32]{1,0:T(1,128)S(1)} %bitcast.3, s32[1,32]{1,0:T(1,128)S(1)} %copy-done.12, bf16[1,3,128,1024]{3,2,1,0:T(8,128)(2,1)S(1)} %copy-done.1, bf16[1,128,1024]{2,1,0:T(8,128)(2,1)S(1)} %copy-done.3, ...), custom_call_target="tpu_custom_call" | custom-call | tf_op jit(solution)/shard_map/encode/pallas_call | solution.py:247
  10.9 0.0 copy-start
  11.0 0.0 copy-start.2
  11.0 0.0 copy-start.4
  11.0 71.0 %merge.1 = bf16[256,4,128]{2,1,0:T(4,128)(2,1)S(1)} custom-call(bf16[256,24,128]{2,1,0:T(8,128)(2,1)S(1)} %encode.1.msg_ref), custom_call_target="tpu_custom_call" | custom-call | tf_op jit(solution)/shard_map/merge/pallas_call | solution.py:449
  81.9 0.0 copy-done.5
  82.0 0.0 copy-done.6
  82.0 0.0 copy-done.7
  82.0 0.0 copy-done.8
  82.0 0.0 copy-done.9
  82.0 0.0 copy-done.10
  82.0 0.0 copy-done
  82.0 0.0 copy-done.2
  82.0 0.0 copy-done.4
  82.0 3.6 %collapse.1 = f32[4,3,4096]{2,1,0:T(4,128)S(1)} custom-call(bf16[1024,128]{1,0:T(8,128)(2,1)S(1)} %bitcast.2, bf16[64,1024]{1,0:T(8,128)(2,1)S(1)} %copy-done.8, bf16[64,256]{1,0:T(8,128)(2,1)S(1)} %copy-done.10, bf16[128,128]{1,0:T(8,128)(2,1)S(1)} %copy-done.9, bf16[128,1024]{1,0:T(8,128)(2,1)S(1)} %copy-done.7, bf16[128,1024]{1,0:T(8,128)(2,1)S(1)} %copy-done.6, ...), custom_call_target="tpu_custom_call" | custom-call | tf_op jit(solution)/shard_map/collapse/pallas_call | solution.py:586
  85.7 0.8 copy.18
Async XLA Ops:
  2.2 1.1 %copy-start.1 = (bf16[1,3,128,1024]{3,2,1,0:T(8,128)(2,1)S(1)}, bf16[1,3,128,1024]{3,2,1,0:T(8,128)(2,1)}, u32[]{:S(2)}) copy-start(bf16[1,3,128,1024]{3,2,1,0:T(8,128)(2,1)} %frames_ref.1) | copy-start | bytes 2359300
  3.3 0.9 %copy-start.3 = (bf16[1,128,1024]{2,1,0:T(8,128)(2,1)S(1)}, bf16[1,128,1024]{2,1,0:T(8,128)(2,1)}, u32[]{:S(2)}) copy-start(bf16[1,128,1024]{2,1,0:T(8,128)(2,1)} %weight_ref.1) | copy-start | bytes 786436
  4.2 0.7 copy-start.11
  4.9 0.7 copy-start.12
  5.6 76.4 %copy-start.5 = (bf16[128,1024]{1,0:T(8,128)(2,1)S(1)}, bf16[128,1024]{1,0:T(8,128)(2,1)}, u32[]{:S(2)}) copy-start(bf16[128,1024]{1,0:T(8,128)(2,1)} %constant.23.clone.spread2) | copy-start | bytes 786436
  5.6 76.4 %copy-start.6 = (bf16[128,1024]{1,0:T(8,128)(2,1)S(1)}, bf16[128,1024]{1,0:T(8,128)(2,1)}, u32[]{:S(2)}) copy-start(bf16[128,1024]{1,0:T(8,128)(2,1)} %constant.22.clone.spread1) | copy-start | bytes 786436
  5.6 76.4 %copy-start.7 = (bf16[128,1024]{1,0:T(8,128)(2,1)S(1)}, bf16[128,1024]{1,0:T(8,128)(2,1)}, u32[]{:S(2)}) copy-start(bf16[128,1024]{1,0:T(8,128)(2,1)} %constant.21.clone.spread0) | copy-start | bytes 786436
  5.6 76.4 %copy-start.8 = (bf16[64,1024]{1,0:T(8,128)(2,1)S(1)}, bf16[64,1024]{1,0:T(8,128)(2,1)}, u32[]{:S(2)}) copy-start(bf16[64,1024]{1,0:T(8,128)(2,1)} %constant.18.clone.lead0) | copy-start | bytes 393220
  5.6 76.4 %copy-start.9 = (bf16[128,128]{1,0:T(8,128)(2,1)S(1)}, bf16[128,128]{1,0:T(8,128)(2,1)}, u32[]{:S(2)}) copy-start(bf16[128,128]{1,0:T(8,128)(2,1)} %constant.20.clone.lead2) | copy-start | bytes 98308
  5.6 76.4 %copy-start.10 = (bf16[64,256]{1,0:T(8,128)(2,1)S(1)}, bf16[64,256]{1,0:T(8,128)(2,1)}, u32[]{:S(2)}) copy-start(bf16[64,256]{1,0:T(8,128)(2,1)} %constant.19.clone.lead1) | copy-start | bytes 98308
  10.9 71.1 %copy-start = (f32[256,1024]{1,0:T(8,128)S(1)}, f32[256,1024]{1,0:T(8,128)}, u32[]{:S(2)}) copy-start(f32[256,1024]{1,0:T(8,128)} %constant.25.clone.wide1) | copy-start | bytes 3145732
  11.0 71.1 %copy-start.2 = (f32[128,1024]{1,0:T(8,128)S(1)}, f32[128,1024]{1,0:T(8,128)}, u32[]{:S(2)}) copy-start(f32[128,1024]{1,0:T(8,128)} %constant.26.clone.wide2) | copy-start | bytes 1572868
  11.0 71.1 %copy-start.4 = (f32[256,256]{1,0:T(8,128)S(1)}, f32[256,256]{1,0:T(8,128)}, u32[]{:S(2)}) copy-start(f32[256,256]{1,0:T(8,128)} %constant.24.clone.keep0) | copy-start | bytes 786436

commit v4 on v3

--- a/solution.py
+++ b/solution.py
@@ -35,8 +35,8 @@
     return (a + e) * (1.0 / 16.0) + (b + d) * 0.25 + c * 0.375
 
 
-def encode_kernel(
-    cell_ref, partner_ref, group_ref, position_ref, frames_ref, weight_ref, mask_ref, out_ref, perm, zbuf, lev0, half, tail, *levs
+def encode_part(
+    cell_ref, partner_ref, group_ref, position_ref, frames_ref, weight_ref, mask_ref, out_ref, perm, zbuf, lev0, half, tail, levs
 ):
     cell = cell_ref[0]
     sub = iota((8, 128), 0)
@@ -134,7 +134,7 @@
         place(img)
     km = iota((64, 1), 0)
     strip_perm = ((km % 16 == nu // 64) & (nu % 64 == cell + km // 16)).astype(F32).astype(BF16)
-    zbuf[...] = dot(dot(order, mask_ref[0].astype(F32).astype(BF16)).astype(BF16), strip_perm)
+    zbuf[...] = dot(dot_t(order, mask_ref[0].astype(F32).astype(BF16)).astype(BF16), strip_perm)
     place(4)
 
     first, last = grp == 0, grp == 63
@@ -242,26 +242,6 @@
         out_ref[d, 16:24, :] = tail[d * 8 : d * 8 + 8, :].astype(BF16)
 
 
-def encode(cell, partner, group, position, frames, weight, mask):
-    vmem = pl.BlockSpec(memory_space=pltpu.VMEM)
-    return pl.pallas_call(
-        encode_kernel,
-        out_shape=jax.ShapeDtypeStruct((DEV, ROWS, 128), BF16),
-        in_specs=[pl.BlockSpec(memory_space=pltpu.SMEM)] * 2 + [vmem] * 5,
-        out_specs=vmem,
-        scratch_shapes=[
-            pltpu.VMEM((1024, 1024), BF16),
-            pltpu.VMEM((128, 1024), F32),
-            pltpu.VMEM((5, 8, 16, 8, 128), F32),
-            pltpu.VMEM((8, 16, 8, 128), F32),
-            pltpu.VMEM((DEV * 8, 128), F32),
-        ]
-        + [pltpu.VMEM((5, max(8 >> k, 1), 16 >> k, 8, 128), F32) for k in range(1, 5)],
-        compiler_params=pltpu.CompilerParams(vmem_limit_bytes=48 << 20),
-        name="encode",
-    )(cell, partner, group, position, frames, weight, mask)
-
-
 def one_hot(high, low):
     n = high.shape[1]
     here = (jnp.broadcast_to(low, (16, n)).astype(I32) == iota((16, n), 0)).astype(F32).astype(BF16)
@@ -270,37 +250,111 @@
     return jnp.concatenate([jnp.where(high == jnp.full((16, n), t, BF16), here, zero) for t in range(GROUPS)], axis=0)
 
 
-def place_of(p):
-    return (p // 4, p % 4)
-
-
-def merge_kernel(
-    msg_ref, out_ref, got, table, tail, ids, acc, wide, sums, send1, recv1, own1, send2, recv2, own2
+MESH_ID = pl.DeviceIdType.MESH
+
+
+def blend_kernel(
+    cell_ref,
+    partner_ref,
+    group_hbm,
+    position_hbm,
+    frames_hbm,
+    weight_hbm,
+    mask_hbm,
+    *rest,
 ):
-    me = lax.axis_index("frames") * 4 + lax.axis_index("tiles")
+    tables_hbm, rest = rest[:9], rest[9:]
+    out_ref, rest = rest[0], rest[1:]
+    tables, rest = rest[:9], rest[9:]
+    (
+    group,
+    position,
+    frames,
+    weight,
+    mask,
+    loaded,
+    msg_ref,
+    perm,
+    zbuf,
+    lev0,
+    half,
+    lev1,
+    lev2,
+    lev3,
+    lev4,
+    flat,
+    got,
+    table,
+    tail,
+    ids,
+    acc,
+    wide,
+    sums,
+    send1,
+    recv1,
+    own1,
+    send2,
+    recv2,
+    own2,
+    back,
+    pic,
+    loaded2,
+    ) = rest
+    loads = [
+        pltpu.make_async_copy(src, dst, loaded.at[i])
+        for i, (src, dst) in enumerate(
+            ((frames_hbm, frames), (weight_hbm, weight), (mask_hbm, mask), (group_hbm, group), (position_hbm, position))
+        )
+    ]
+    for load in loads:
+        load.start()
+    table_loads = [
+        pltpu.make_async_copy(src, dst, loaded2.at[i]) for i, (src, dst) in enumerate(zip(tables_hbm, tables))
+    ]
+    for load in table_loads:
+        load.start()
+    me_f, me_t = lax.axis_index("frames"), lax.axis_index("tiles")
+    me = me_f * 4 + me_t
     barrier = pltpu.get_barrier_semaphore()
 
-    @pl.loop(1, DEV)
-    def _(i):
-        pl.semaphore_signal(
-            barrier, inc=1, device_id=place_of((me + i) % DEV), device_id_type=pl.DeviceIdType.MESH
-        )
-
+    def peers(visit):
+        for dt in range(1, 4):
+            visit(me_f, lax.rem(me_t + dt, 4))
+
+        @pl.loop(1, 32)
+        def _(i):
+            for f in (lax.rem(me_f + i, 64), lax.rem(me_f + 64 - i, 64)):
+                for dt in range(4):
+                    visit(f, lax.rem(me_t + dt, 4))
+
+        for dt in range(4):
+            visit(lax.rem(me_f + 32, 64), lax.rem(me_t + dt, 4))
+
+    def greet(f, t):
+        pl.semaphore_signal(barrier, inc=1, device_id=(f, t), device_id_type=MESH_ID)
+
+    peers(greet)
+    for load in loads:
+        load.wait()
+    encode_part(
+        cell_ref, partner_ref, group, position, frames, weight, mask, msg_ref, perm, zbuf, lev0, half, flat,
+        (lev1, lev2, lev3, lev4),
+    )
     pl.semaphore_wait(barrier, DEV - 1)
     keep1 = pltpu.make_async_copy(msg_ref.at[me], got.at[me], own1)
     keep1.start()
 
-    @pl.loop(1, DEV)
-    def _(i):
-        peer = (me + i) % DEV
+    def deliver(f, t):
         pltpu.make_async_remote_copy(
-            src_ref=msg_ref.at[peer],
+            src_ref=msg_ref.at[f * 4 + t],
             dst_ref=got.at[me],
             send_sem=send1,
-            recv_sem=recv1.at[me // 16],
-            device_id=place_of(peer),
-            device_id_type=pl.DeviceIdType.MESH,
+            recv_sem=recv1.at[me_f // 4],
+            device_id=(f, t),
+            device_id_type=MESH_ID,
         ).start()
+
+    peers(deliver)
 
     lane = iota((8, 128), 1)
     bit1, bit0 = lane // 2 % 2 == 0, lane % 2 == 0
@@ -341,17 +395,22 @@
             datas.append(table[4 * j + s])
         acc[...] += dot_t(jnp.concatenate(hots, axis=1), jnp.concatenate(datas, axis=1))
 
-    @pl.loop(1, 16)
-    def _(k):
-        j = (me // 16 + 16 - k) % 16
+    keep1.wait()
+    some = got.at[pl.ds(0, 15)]
+    pltpu.make_async_copy(some, some, recv1.at[me_f // 4]).wait()
+    add_block(me_f // 4)
+
+    def take(j):
         some = got.at[pl.ds(0, 16)]
         pltpu.make_async_copy(some, some, recv1.at[j]).wait()
         add_block(j)
 
-    keep1.wait()
-    some = got.at[pl.ds(0, 15)]
-    pltpu.make_async_copy(some, some, recv1.at[me // 16]).wait()
-    add_block(me // 16)
+    @pl.loop(1, 8)
+    def _(k):
+        take(lax.rem(me_f // 4 + k, 16))
+        take(lax.rem(me_f // 4 + 16 - k, 16))
+
+    take(lax.rem(me_f // 4 + 8, 16))
 
     p0 = tail[:, 6, :]
     p1 = tail[:, 7, :]
@@ -422,36 +481,56 @@
         wide[:, t, :] = total / jnp.maximum(den, 1.0)
     sums[...] = wide[...].astype(BF16)
 
-    keep2 = pltpu.make_async_copy(sums.at[me], out_ref.at[me], own2)
+    keep2 = pltpu.make_async_copy(sums.at[me], back.at[me], own2)
     keep2.start()
 
-    @pl.loop(1, DEV)
-    def _(i):
-        peer = (me + i) % DEV
+    def answer(f, t):
         pltpu.make_async_remote_copy(
-            src_ref=sums.at[peer],
-            dst_ref=out_ref.at[me],
+            src_ref=sums.at[f * 4 + t],
+            dst_ref=back.at[me],
             send_sem=send2,
             recv_sem=recv2,
-            device_id=place_of(peer),
-            device_id_type=pl.DeviceIdType.MESH,
+            device_id=(f, t),
+            device_id_type=MESH_ID,
         ).start()
 
+    peers(answer)
+    for load in table_loads:
+        load.wait()
     keep2.wait()
-    for ref, sem in ((msg_ref, send1), (sums, send2), (out_ref, recv2)):
+    for ref, sem in ((msg_ref, send1), (sums, send2), (back, recv2)):
         some = ref.at[pl.ds(0, DEV - 1)]
         pltpu.make_async_copy(some, some, sem).wait()
-
-
-def merge(msg):
-    vmem = pl.BlockSpec(memory_space=pltpu.VMEM)
+    wide[...] = back[...].astype(F32)
+    collapse_part(wide, *tables, out_ref, pic)
+
+
+def blend(cell, partner, group, position, frames, weight, mask):
+    vmem, smem, hbm = (pl.BlockSpec(memory_space=m) for m in (pltpu.VMEM, pltpu.SMEM, pltpu.HBM))
     one = pltpu.SemaphoreType.DMA
+    tables = [jnp.asarray(t) for t in collapse_tables()]
     return pl.pallas_call(
-        merge_kernel,
-        out_shape=jax.ShapeDtypeStruct((DEV, 4, 128), BF16),
-        in_specs=[vmem],
+        blend_kernel,
+        out_shape=jax.ShapeDtypeStruct((3, 4, 4096), F32),
+        in_specs=[smem, smem] + [hbm] * 14,
         out_specs=vmem,
-        scratch_shapes=[
+        scratch_shapes=[pltpu.VMEM(t.shape, t.dtype) for t in tables]
+        + [
+            pltpu.VMEM((1, 32), I32),
+            pltpu.VMEM((1, 32), I32),
+            pltpu.VMEM((1, 3, 128, 1024), BF16),
+            pltpu.VMEM((1, 128, 1024), BF16),
+            pltpu.VMEM((1, 64, 128), I32),
+            pltpu.SemaphoreType.DMA((5,)),
+            pltpu.VMEM((DEV, ROWS, 128), BF16),
+            pltpu.VMEM((1024, 1024), BF16),
+            pltpu.VMEM((128, 1024), F32),
+            pltpu.VMEM((5, 8, 16, 8, 128), F32),
+            pltpu.VMEM((8, 16, 8, 128), F32),
+        ]
+        + [pltpu.VMEM((5, max(8 >> k, 1), 16 >> k, 8, 128), F32) for k in range(1, 5)]
+        + [
+            pltpu.VMEM((DEV * 8, 128), F32),
             pltpu.VMEM((DEV, ROWS, 128), BF16),
             pltpu.VMEM((GROUPS, 128, 128), BF16),
             pltpu.VMEM((DEV, 8, 128), F32),
@@ -465,10 +544,13 @@
             one,
             one,
             one,
+            pltpu.VMEM((DEV, 4, 128), BF16),
+            pltpu.VMEM((3, 32, 128), F32),
+            pltpu.SemaphoreType.DMA((9,)),
         ],
-        compiler_params=pltpu.CompilerParams(collective_id=1, has_side_effects=True, vmem_limit_bytes=48 << 20),
-        name="merge",
-    )(msg)
+        compiler_params=pltpu.CompilerParams(collective_id=1, has_side_effects=True, vmem_limit_bytes=60 << 20),
+        name="blend",
+    )(cell, partner, group, position, frames, weight, mask, *tables)
 
 
 def grow_matrices():
@@ -542,14 +624,11 @@
     return high, (x - high.astype(F32)).astype(BF16)
 
 
-def collapse_kernel(
-    msg_ref, lead0, lead1, lead2, spread0, spread1, spread2, keep0, wide1, wide2, out_ref, buf, pic
-):
-    buf[...] = msg_ref[...].astype(F32)
+def collapse_part(wide, lead0, lead1, lead2, spread0, spread1, spread2, keep0, wide1, wide2, out_ref, pic):
     ln = iota((128, 128), 1)
     low = iota((32, 128), 1) < 64
     for t in range(4):
-        x = buf[pl.ds(t, 256, stride=4), :]
+        x = wide[:, t, :]
         xb = x.astype(BF16)
         fine = dot(xb, spread0[...])
         total = jnp.zeros((64, 256), F32)
@@ -577,29 +656,20 @@
         pic[2] = jnp.where(low, even[:, 128:256], pltpu.roll(odd[:, 128:256], 64, 1))
         for m in range(32):
             for c in range(3):
-                out_ref[t, c : c + 1, m * 128 : m * 128 + 128] = pic[c, m : m + 1, :]
-
-
-def collapse(msg):
-    vmem = pl.BlockSpec(memory_space=pltpu.VMEM)
-    tables = [jnp.asarray(t) for t in collapse_tables()]
-    return pl.pallas_call(
-        collapse_kernel,
-        out_shape=jax.ShapeDtypeStruct((4, 3, 4096), F32),
-        in_specs=[vmem] * (1 + len(tables)),
-        out_specs=vmem,
-        scratch_shapes=[pltpu.VMEM((1024, 128), F32), pltpu.VMEM((3, 32, 128), F32)],
-        compiler_params=pltpu.CompilerParams(vmem_limit_bytes=48 << 20),
-        name="collapse",
-    )(msg, *tables)
+                out_ref[c, t : t + 1, m * 128 : m * 128 + 128] = pic[c, m : m + 1, :]
 
 
 def local(frames, weight_map, seam_mask, strip_cell, partner, tile_group, tile_position_in_group):
-    sent = encode(
-        strip_cell, partner, tile_group.reshape(1, 32), tile_position_in_group, frames, weight_map, seam_mask
+    picture = blend(
+        strip_cell,
+        partner,
+        tile_group.reshape(1, 32),
+        tile_position_in_group,
+        frames,
+        weight_map,
+        seam_mask.transpose(0, 2, 1),
     )
-    back = merge(sent)
-    return collapse(back.reshape(TILES, 128))
+    return picture.transpose(1, 0, 2)
 
 
 def solution(mesh):

time: 86.7 us -> 79.7 us (0.919)
  local copies, waits for them, and re-layouts: 5.09 us -> 1.62 us
  Pallas kernels: 79.9 us -> 76.7 us
    pallas_call x3 -> x1, Pallas kernels: 79.9 us -> 76.7 us  [blend(): pl.pallas_call(blend_kernel, out_shape=jax.ShapeDtypeStruct((3, 4, 4096),...]
    unnamed x27 -> x1, local copies, waits for them, and re-layouts: 4.29 us -> 1.62 us
where the time goes in v4:
time: 79.7 us; the launch traced here: 79.6 us
  Pallas kernels  76.7 us (96%)
  local copies, waits for them, and re-layouts  1.62 us (2%)
  between operations  1.31 us (2%)
    pallas_call x1, Pallas kernels, blend(): pl.pallas_call(blend_kernel, out_shape=jax.ShapeDtypeStruct((3, 4, 4096),...  76.7 us
    unnamed x1, local copies, waits for them, and re-layouts  1.62 us

profile of v4, /device:TPU:1, one launch (start us, length us, event | category | flops | bytes accessed | tf_op | source)
XLA Modules:
  0.0 79.6 jit_solution(18327556226248664441)
XLA Ops:
  1.3 76.7 %blend.1 = f32[3,4,4096]{2,1,0:T(4,128)} custom-call(s32[1]{0:T(128)S(6)} %copy.18.cell_ref, s32[1]{0:T(128)S(6)} %copy.19.partner_ref, s32[1,32]{1,0:T(1,128)} %bitcast.5, s32[1,32]{1,0:T(1,128)} %position_hbm.1, bf16[1,3,128,1024]{3,2,1,0:T(8,128)(2,1)} %frames_hbm.1, bf16[1,128,1024]{2,1,0:T(8,128)(2,1)} %weight_hbm.1, s32[1,64,128]{2,1,0:T(8,128)} %bitcast.4, ...), custom_call_target="tpu_custom_call" | custom-call | tf_op jit(solution)/shard_map/blend/pallas_call | solution.py:512
  78.0 1.6 %copy.20 = f32[4,3,4096]{2,0,1:T(4,128)} copy(f32[4,3,4096]{2,0,1:T(4,128)} %bitcast.3) | data formatting | bytes 393216

commit v5 on v4

--- a/solution.py
+++ b/solution.py
@@ -229,15 +229,16 @@
                     tail[pl.ds(base + 7, 8, stride=8), :] = old + u
                 else:
                     c = {2: r * 4 + a, 3: 8 + a, 4: 10}[k]
-                    for p in range(2):
-                        base = (p * 128 + c * 8) * 8
-                        for e in range(2):
-                            tail[pl.ds(base + 4 + e, 8, stride=8), :] = data[2 * p + e]
-                        u = jnp.where(slot1 == 4, picked[2 * p], 0.0)
-                        if p == 0:
-                            u = jnp.where(slot1 == 5, picked[1], u)
+                    for ch in range(3):
+                        base = (ch * 84 + c * 8) * 8
+                        u = jnp.where(slot1 == 4, picked[ch], 0.0)
                         u = jnp.where(slot1 == 6, picked[3], u)
-                        tail[pl.ds(base + 7, 8, stride=8), :] = u
+                        for row, value in ((4, data[ch]), (5, data[3]), (7, u)):
+                            if k < 4:
+                                tail[pl.ds(base + row, 8, stride=8), :] = value
+                            else:
+                                for e in range(4):
+                                    tail[pl.ds(base + e * 8 + row, 1), :] = value[2 * e : 2 * e + 1]
     for d in range(DEV):
         out_ref[d, 16:24, :] = tail[d * 8 : d * 8 + 8, :].astype(BF16)
 
@@ -473,12 +474,19 @@
 
     ln = iota((DEV, 128), 1)
     r = ln % 32
+    normal = []
     for t in range(4):
         total = acc[t * DEV : t * DEV + DEV, :]
         den = jnp.ones((DEV, 128), F32)
-        for low, high, by in ((0, 4, 12), (4, 8, 8), (8, 12, 4), (16, 17, 3), (17, 18, 2), (18, 19, 1)):
+        for low, high, by in ((0, 4, 12), (4, 8, 8), (8, 12, 4), (16, 17, 3), (17, 18, 2), (18, 19, 1), (20, 21, 1)):
             den = jnp.where((r >= low) & (r < high), pltpu.roll(total, 128 - by, 1), den)
-        wide[:, t, :] = total / jnp.maximum(den, 1.0)
+        normal.append((total / jnp.maximum(den, 1.0)).astype(BF16))
+    kc, nc = iota((256, 1), 0), iota((1, 128), 1)
+    slim = nc % 16
+    slim = jnp.where(slim < 12, slim, jnp.where(slim < 15, slim + 4, 20))
+    keep = (kc == nc // 64 * 128 + nc % 64 // 16 * 32 + slim).astype(F32).astype(BF16)
+    for u in range(2):
+        wide[:, u, :] = dot(jnp.concatenate(normal[2 * u : 2 * u + 2], axis=1), keep)
     sums[...] = wide[...].astype(BF16)
 
     keep2 = pltpu.make_async_copy(sums.at[me], back.at[me], own2)
@@ -536,16 +544,16 @@
             pltpu.VMEM((DEV, 8, 128), F32),
             pltpu.VMEM((2, GROUPS, 128), F32),
             pltpu.VMEM((TILES, 128), F32),
-            pltpu.VMEM((DEV, 4, 128), F32),
-            pltpu.VMEM((DEV, 4, 128), BF16),
+            pltpu.VMEM((DEV, 2, 128), F32),
+            pltpu.VMEM((DEV, 2, 128), BF16),
             one,
             pltpu.SemaphoreType.DMA((16,)),
             one,
             one,
             one,
             one,
-            pltpu.VMEM((DEV, 4, 128), BF16),
-            pltpu.VMEM((3, 32, 128), F32),
+            pltpu.VMEM((DEV, 2, 128), BF16),
+            pltpu.VMEM((2, 64, 128), F32),
             pltpu.SemaphoreType.DMA((9,)),
         ],
         compiler_params=pltpu.CompilerParams(collective_id=1, has_side_effects=True, vmem_limit_bytes=60 << 20),
@@ -572,51 +580,35 @@
     d = np.arange(256)
     h, a0, r0 = d % 2, d // 2 % 16, d // 32
     rs1, a1, r1 = d % 8, d // 8 % 8, d // 64
-    pic = np.concatenate([np.arange(0, 64, 2), np.arange(1, 64, 2)])
-    lead0 = np.zeros((64, 4, 256), np.float32)
-    for j in range(4):
-        row = (h * 4 + j) * 8 + r0
-        lead0[:, j, :] = pic[:, None] == row[None, :]
-    lead1 = gam[1][pic][:, rs1 * 4 + r1].astype(np.float32)
+    lead0 = np.arange(16)[:, None] == (h * 8 + r0)[None, :]
+    lead1 = gam[1][:, rs1 * 4 + r1]
     wide1 = np.zeros((256, 4, 64), np.float32)
     for g in range(4):
         wide1[:, g, :] = gam[1][:, g * 8 + a1].T
-    lead2 = np.zeros((64, 128), np.float32)
-    wide2 = np.zeros((128, 4, 64), np.float32)
-    for p in range(88):
-        c, rs = p // 8, p % 8
+    wide1 = np.tile(wide1, (1, 1, 4)).reshape(256, 1024)
+    lead2 = np.zeros((64, 256), np.float32)
+    wide2 = np.zeros((256, 4, 64), np.float32)
+    for p in range(252):
+        c, rs = p % 84 // 8, p % 8 if p < 84 else p % 84 % 8
         if c < 8:
             k, row, col, step = 2, rs * 2 + c // 4, c % 4, 4
         elif c < 10:
             k, row, col, step = 3, rs, c - 8, 2
-        elif rs % 2 == 0:
-            k, row, col, step = 4, rs // 2, 0, 1
         else:
-            continue
-        lead2[:, p] = gam[k][pic, row]
+            k, row, col, step = 4, rs, 0, 1
+        lead2[:, p] = gam[k][:, row]
         for g in range(4):
             wide2[p, g, :] = gam[k][:, g * step + col]
-    wide1 = np.tile(wide1, (1, 1, 4)).astype(np.float32)
-    wide2 = np.tile(wide2, (1, 1, 4)).astype(np.float32)
     lead2_high = lead2.astype(jnp.bfloat16)
     lead2_low = (lead2 - lead2_high.astype(np.float32)).astype(jnp.bfloat16)
     lane, nu = np.arange(128)[:, None], np.arange(1024)[None, :]
     ch, col, j = nu % 256 // 64, nu % 64, nu // 256
-    spread0 = ((lane == (col // 16) * 32 + ch * 4 + j) & (ch < 3)).astype(jnp.bfloat16)
-    spread1 = ((lane == j * 32 + 16 + ch) & (ch < 3)).astype(jnp.bfloat16)
-    spread2 = ((lane == j * 32 + 20 + ch) & (ch < 3)).astype(jnp.bfloat16)
-    keep0 = (a0[:, None] == np.arange(256)[None, :] % 16).astype(np.float32)
-    return (
-        lead0.reshape(64, 1024).astype(jnp.bfloat16),
-        lead1.astype(jnp.bfloat16),
-        np.concatenate([lead2_high, lead2_low], axis=0),
-        spread0,
-        spread1,
-        spread2,
-        keep0,
-        wide1.reshape(256, 1024),
-        wide2.reshape(128, 1024),
-    )
+    spread0 = (lane == (col // 16) * 16 + ch * 4 + j) & (ch < 3)
+    spread1 = (lane == j * 16 + 12 + ch) & (ch < 3)
+    spread2 = lane == np.arange(256)[None, :] // 64 * 16 + 15
+    keep0 = a0[:, None] == np.arange(256)[None, :] % 16
+    low = [t.astype(jnp.bfloat16) for t in (lead0, lead1, spread0, spread1, spread2, keep0, wide1)]
+    return (*low, np.concatenate([lead2_high, lead2_low], axis=0), wide2.reshape(256, 256))
 
 
 def split(x):
@@ -624,39 +616,41 @@
     return high, (x - high.astype(F32)).astype(BF16)
 
 
-def collapse_part(wide, lead0, lead1, lead2, spread0, spread1, spread2, keep0, wide1, wide2, out_ref, pic):
-    ln = iota((128, 128), 1)
+def collapse_part(wide, lead0, lead1, spread0, spread1, spread2, keep0, wide1, lead2, wide2, out_ref, pic):
     low = iota((32, 128), 1) < 64
+    channel = (iota((256, 256), 0) // 84 == iota((256, 256), 1) // 64).astype(F32)
     for t in range(4):
-        x = wide[:, t, :]
-        xb = x.astype(BF16)
-        fine = dot(xb, spread0[...])
-        total = jnp.zeros((64, 256), F32)
+        x = wide[:, t // 2, :]
+        if t % 2:
+            x = pltpu.roll(x, 64, 1)
+        x = x.astype(BF16)
+        fine = []
         for j in range(4):
-            part = (fine[:, j * 256 : j * 256 + 256] * keep0[...]).astype(BF16)
-            total = total + dot(lead0[:, j * 256 : j * 256 + 256], part)
-        mid = dot(xb, spread1[...]) * wide1[...]
-        mid = (mid[:, 0:256] + mid[:, 256:512]) + (mid[:, 512:768] + mid[:, 768:1024])
+            part = dot(x, spread0[:, j * 256 : j * 256 + 256]).astype(BF16) * keep0[...]
+            fine.append(dot(lead0[...], part))
+        total = jnp.concatenate([fine[j][h * 8 : h * 8 + 8] for h in range(2) for j in range(4)], axis=0)
+        mid = jnp.zeros((256, 256), F32)
+        for g in range(4):
+            some = slice(g * 256, g * 256 + 256)
+            mid = mid + dot(x, spread1[:, some]) * wide1[:, some].astype(F32)
         mh, ml = split(mid)
         total = total + dot(lead1[...], mh) + dot(lead1[...], ml)
-        up, down = x[0:128], x[128:256]
-        weight = pltpu.roll(down, 127, 1)
-        nu = up / jnp.maximum(jnp.where(ln % 32 == 20, weight, down), 1.0)
-        nd = down / jnp.maximum(weight, 1.0)
-        coarse = jnp.where(ln % 32 == 22, pltpu.roll(nd, 2, 1), nu)
-        coarse = jnp.where((ln % 32 >= 20) & (ln % 32 < 23), coarse, 0.0)
-        ch, cl = split(coarse)
-        far = (dot(ch, spread2[...]) + dot(cl, spread2[...])) * wide2[...]
-        far = (far[:, 0:256] + far[:, 256:512]) + (far[:, 512:768] + far[:, 768:1024])
-        fh, fl = split(far)
+        far = dot(x, spread2[...]) * wide2[...]
+        far = far[:, :128] + far[:, 128:]
+        far = far + pltpu.roll(far, 64, 1)
+        fh, fl = split(jnp.concatenate([far, far], axis=1) * channel)
         total = total + dot(lead2[0:64], fh) + dot(lead2[64:128], fh) + dot(lead2[0:64], fl)
-        even, odd = total[0:32], total[32:64]
-        pic[0] = jnp.where(low, even[:, 0:128], pltpu.roll(odd[:, 0:128], 64, 1))
-        pic[1] = jnp.where(low, pltpu.roll(even[:, 0:128], 64, 1), odd[:, 0:128])
-        pic[2] = jnp.where(low, even[:, 128:256], pltpu.roll(odd[:, 128:256], 64, 1))
-        for m in range(32):
-            for c in range(3):
-                out_ref[c, t : t + 1, m * 128 : m * 128 + 128] = pic[c, m : m + 1, :]
+        pic[0], pic[1] = total[:, :128], total[:, 128:]
+        even = [pic[i, pl.ds(0, 32, stride=2), :] for i in range(2)]
+        odd = [pic[i, pl.ds(1, 32, stride=2), :] for i in range(2)]
+        pairs = (
+            jnp.where(low, even[0], pltpu.roll(odd[0], 64, 1)),
+            jnp.where(low, pltpu.roll(even[0], 64, 1), odd[0]),
+            jnp.where(low, even[1], pltpu.roll(odd[1], 64, 1)),
+        )
+        for c in range(3):
+            for m in range(32):
+                out_ref[c, t : t + 1, m * 128 : m * 128 + 128] = pairs[c][m : m + 1]
 
 
 def local(frames, weight_map, seam_mask, strip_cell, partner, tile_group, tile_position_in_group):

time: 79.7 us -> 78.5 us (0.985)
  Pallas kernels: 76.7 us -> 75.5 us
    pallas_call x1, Pallas kernels: 76.7 us -> 75.5 us  [blend(): pl.pallas_call(blend_kernel, out_shape=jax.ShapeDtypeStruct((3, 4, 4096),...]
where the time goes in v5:
time: 78.5 us; the launch traced here: 78.4 us
  Pallas kernels  75.5 us (96%)
  local copies, waits for them, and re-layouts  1.62 us (2%)
  between operations  1.31 us (2%)
    pallas_call x1, Pallas kernels, blend(): pl.pallas_call(blend_kernel, out_shape=jax.ShapeDtypeStruct((3, 4, 4096),...  75.5 us
    unnamed x1, local copies, waits for them, and re-layouts  1.62 us

profile of v5, /device:TPU:1, one launch (start us, length us, event | category | flops | bytes accessed | tf_op | source)
XLA Modules:
  0.0 78.4 jit_solution(2580798023856255757)
XLA Ops:
  1.3 75.5 %blend.1 = f32[3,4,4096]{2,1,0:T(4,128)} custom-call(s32[1]{0:T(128)S(6)} %copy.18.cell_ref, s32[1]{0:T(128)S(6)} %copy.19.partner_ref, s32[1,32]{1,0:T(1,128)} %bitcast.5, s32[1,32]{1,0:T(1,128)} %position_hbm.1, bf16[1,3,128,1024]{3,2,1,0:T(8,128)(2,1)} %frames_hbm.1, bf16[1,128,1024]{2,1,0:T(8,128)(2,1)} %weight_hbm.1, s32[1,64,128]{2,1,0:T(8,128)} %bitcast.4, ...), custom_call_target="tpu_custom_call" | custom-call | tf_op jit(solution)/shard_map/blend/pallas_call | solution.py:520
  76.8 1.6 %copy.20 = f32[4,3,4096]{2,0,1:T(4,128)} copy(f32[4,3,4096]{2,0,1:T(4,128)} %bitcast.3) | data formatting | bytes 393216

commit v6 on v5

--- a/solution.py
+++ b/solution.py
@@ -300,6 +300,8 @@
     back,
     pic,
     loaded2,
+    send0,
+    recv0,
     ) = rest
     loads = [
         pltpu.make_async_copy(src, dst, loaded.at[i])
@@ -345,16 +347,29 @@
     keep1 = pltpu.make_async_copy(msg_ref.at[me], got.at[me], own1)
     keep1.start()
 
+    fine, side = pl.ds(0, 16), pl.ds(16, 8)
+
+    def deliver_side(f, t):
+        pltpu.make_async_remote_copy(
+            src_ref=msg_ref.at[f * 4 + t, side],
+            dst_ref=got.at[me, side],
+            send_sem=send0,
+            recv_sem=recv0,
+            device_id=(f, t),
+            device_id_type=MESH_ID,
+        ).start()
+
     def deliver(f, t):
         pltpu.make_async_remote_copy(
-            src_ref=msg_ref.at[f * 4 + t],
-            dst_ref=got.at[me],
+            src_ref=msg_ref.at[f * 4 + t, fine],
+            dst_ref=got.at[me, fine],
             send_sem=send1,
             recv_sem=recv1.at[me_f // 4],
             device_id=(f, t),
             device_id_type=MESH_ID,
         ).start()
 
+    peers(deliver_side)
     peers(deliver)
 
     lane = iota((8, 128), 1)
@@ -369,8 +384,6 @@
 
     def arrange(j):
         x = [got[4 * j + s].astype(F32) for s in range(4)]
-        for s in range(4):
-            tail[4 * j + s] = x[s][16:24]
         parts = [[], [], [], []]
         for t in range(3):
             v = [x[s][8 * t : 8 * t + 8] for s in range(4)]
@@ -387,31 +400,14 @@
 
     acc[...] = jnp.zeros((TILES, 128), F32)
 
-    def add_block(j):
-        for s in range(4):
-            arrange(4 * j + s)
-        hots, datas = [], []
-        for s in range(4):
-            hots.append(one_hot(ids[0, pl.ds(4 * j + s, 1), :], ids[1, pl.ds(4 * j + s, 1), :]))
-            datas.append(table[4 * j + s])
-        acc[...] += dot_t(jnp.concatenate(hots, axis=1), jnp.concatenate(datas, axis=1))
-
     keep1.wait()
-    some = got.at[pl.ds(0, 15)]
-    pltpu.make_async_copy(some, some, recv1.at[me_f // 4]).wait()
-    add_block(me_f // 4)
-
-    def take(j):
-        some = got.at[pl.ds(0, 16)]
-        pltpu.make_async_copy(some, some, recv1.at[j]).wait()
-        add_block(j)
-
-    @pl.loop(1, 8)
-    def _(k):
-        take(lax.rem(me_f // 4 + k, 16))
-        take(lax.rem(me_f // 4 + 16 - k, 16))
-
-    take(lax.rem(me_f // 4 + 8, 16))
+    some = got.at[pl.ds(0, DEV - 1), side]
+    pltpu.make_async_copy(some, some, recv0).wait()
+
+    @pl.loop(0, GROUPS)
+    def _(j):
+        for i in range(4):
+            tail[4 * j + i] = got[4 * j + i, 16:24, :].astype(F32)
 
     p0 = tail[:, 6, :]
     p1 = tail[:, 7, :]
@@ -472,6 +468,31 @@
         hot = one_hot(*(jnp.where(next_block, v, u) for u, v in zip(under[0][s // 4], under[1][s // 4])))
         acc[...] += dot(hot, extra[:, s * 128 : s * 128 + 128])
 
+    def add_block(j):
+        for s in range(4):
+            arrange(4 * j + s)
+        hots, datas = [], []
+        for s in range(4):
+            hots.append(one_hot(ids[0, pl.ds(4 * j + s, 1), :], ids[1, pl.ds(4 * j + s, 1), :]))
+            datas.append(table[4 * j + s])
+        acc[...] += dot_t(jnp.concatenate(hots, axis=1), jnp.concatenate(datas, axis=1))
+
+    some = got.at[pl.ds(0, 15), fine]
+    pltpu.make_async_copy(some, some, recv1.at[me_f // 4]).wait()
+    add_block(me_f // 4)
+
+    def take(j):
+        some = got.at[pl.ds(0, 16), fine]
+        pltpu.make_async_copy(some, some, recv1.at[j]).wait()
+        add_block(j)
+
+    @pl.loop(1, 8)
+    def _(k):
+        take(lax.rem(me_f // 4 + k, 16))
+        take(lax.rem(me_f // 4 + 16 - k, 16))
+
+    take(lax.rem(me_f // 4 + 8, 16))
+
     ln = iota((DEV, 128), 1)
     r = ln % 32
     normal = []
@@ -506,8 +527,13 @@
     for load in table_loads:
         load.wait()
     keep2.wait()
-    for ref, sem in ((msg_ref, send1), (sums, send2), (back, recv2)):
-        some = ref.at[pl.ds(0, DEV - 1)]
+    others = pl.ds(0, DEV - 1)
+    for some, sem in (
+        (msg_ref.at[others, side], send0),
+        (msg_ref.at[others, fine], send1),
+        (sums.at[others], send2),
+        (back.at[others], recv2),
+    ):
         pltpu.make_async_copy(some, some, sem).wait()
     wide[...] = back[...].astype(F32)
     collapse_part(wide, *tables, out_ref, pic)
@@ -555,6 +581,8 @@
             pltpu.VMEM((DEV, 2, 128), BF16),
             pltpu.VMEM((2, 64, 128), F32),
             pltpu.SemaphoreType.DMA((9,)),
+            one,
+            one,
         ],
         compiler_params=pltpu.CompilerParams(collective_id=1, has_side_effects=True, vmem_limit_bytes=60 << 20),
         name="blend",

time: 78.5 us -> 76 us (0.968)
  Pallas kernels: 75.5 us -> 72.9 us
    pallas_call x1, Pallas kernels: 75.5 us -> 72.9 us  [blend(): pl.pallas_call(blend_kernel, out_shape=jax.ShapeDtypeStruct((3, 4, 4096),...]
where the time goes in v6:
time: 76 us; the launch traced here: 75.8 us
  Pallas kernels  72.9 us (96%)
  local copies, waits for them, and re-layouts  1.62 us (2%)
  between operations  1.31 us (2%)
    pallas_call x1, Pallas kernels, blend(): pl.pallas_call(blend_kernel, out_shape=jax.ShapeDtypeStruct((3, 4, 4096),...  72.9 us
    unnamed x1, local copies, waits for them, and re-layouts  1.62 us

profile of v6, /device:TPU:1, one launch (start us, length us, event | category | flops | bytes accessed | tf_op | source)
XLA Modules:
  0.0 75.8 jit_solution(9776297737953908088)
XLA Ops:
  1.3 72.9 %blend.1 = f32[3,4,4096]{2,1,0:T(4,128)} custom-call(s32[1]{0:T(128)S(6)} %copy.18.cell_ref, s32[1]{0:T(128)S(6)} %copy.19.partner_ref, s32[1,32]{1,0:T(1,128)} %bitcast.5, s32[1,32]{1,0:T(1,128)} %position_hbm.1, bf16[1,3,128,1024]{3,2,1,0:T(8,128)(2,1)} %frames_hbm.1, bf16[1,128,1024]{2,1,0:T(8,128)(2,1)} %weight_hbm.1, s32[1,64,128]{2,1,0:T(8,128)} %bitcast.4, ...), custom_call_target="tpu_custom_call" | custom-call | tf_op jit(solution)/shard_map/blend/pallas_call | solution.py:546
  74.2 1.6 %copy.20 = f32[4,3,4096]{2,0,1:T(4,128)} copy(f32[4,3,4096]{2,0,1:T(4,128)} %bitcast.3) | data formatting | bytes 393216

commit v7 on v6

--- a/solution.py
+++ b/solution.py
@@ -264,9 +264,9 @@
     mask_hbm,
     *rest,
 ):
-    tables_hbm, rest = rest[:9], rest[9:]
+    tables_hbm, rest = rest[:10], rest[10:]
     out_ref, rest = rest[0], rest[1:]
-    tables, rest = rest[:9], rest[9:]
+    tables, rest = rest[:10], rest[10:]
     (
     group,
     position,
@@ -546,7 +546,7 @@
     return pl.pallas_call(
         blend_kernel,
         out_shape=jax.ShapeDtypeStruct((3, 4, 4096), F32),
-        in_specs=[smem, smem] + [hbm] * 14,
+        in_specs=[smem, smem] + [hbm] * 15,
         out_specs=vmem,
         scratch_shapes=[pltpu.VMEM(t.shape, t.dtype) for t in tables]
         + [
@@ -580,7 +580,7 @@
             one,
             pltpu.VMEM((DEV, 2, 128), BF16),
             pltpu.VMEM((2, 64, 128), F32),
-            pltpu.SemaphoreType.DMA((9,)),
+            pltpu.SemaphoreType.DMA((10,)),
             one,
             one,
         ],
@@ -610,10 +610,9 @@
     rs1, a1, r1 = d % 8, d // 8 % 8, d // 64
     lead0 = np.arange(16)[:, None] == (h * 8 + r0)[None, :]
     lead1 = gam[1][:, rs1 * 4 + r1]
-    wide1 = np.zeros((256, 4, 64), np.float32)
-    for g in range(4):
-        wide1[:, g, :] = gam[1][:, g * 8 + a1].T
-    wide1 = np.tile(wide1, (1, 1, 4)).reshape(256, 1024)
+    kc, nc = np.arange(128)[:, None], np.arange(256)[None, :]
+    right1 = gam[1][nc % 64, kc % 32] * (kc // 32 == nc // 64)
+    keep1 = a1[:, None] == np.arange(128)[None, :] % 8
     lead2 = np.zeros((64, 256), np.float32)
     wide2 = np.zeros((256, 4, 64), np.float32)
     for p in range(252):
@@ -632,10 +631,11 @@
     lane, nu = np.arange(128)[:, None], np.arange(1024)[None, :]
     ch, col, j = nu % 256 // 64, nu % 64, nu // 256
     spread0 = (lane == (col // 16) * 16 + ch * 4 + j) & (ch < 3)
-    spread1 = (lane == j * 16 + 12 + ch) & (ch < 3)
+    half = np.arange(128)[None, :]
+    spread1 = (lane == half % 32 // 8 * 16 + 12 + half // 32) & (half < 96)
     spread2 = lane == np.arange(256)[None, :] // 64 * 16 + 15
     keep0 = a0[:, None] == np.arange(256)[None, :] % 16
-    low = [t.astype(jnp.bfloat16) for t in (lead0, lead1, spread0, spread1, spread2, keep0, wide1)]
+    low = [t.astype(jnp.bfloat16) for t in (lead0, lead1, spread0, spread1, spread2, keep0, keep1, right1)]
     return (*low, np.concatenate([lead2_high, lead2_low], axis=0), wide2.reshape(256, 256))
 
 
@@ -644,7 +644,7 @@
     return high, (x - high.astype(F32)).astype(BF16)
 
 
-def collapse_part(wide, lead0, lead1, spread0, spread1, spread2, keep0, wide1, lead2, wide2, out_ref, pic):
+def collapse_part(wide, lead0, lead1, spread0, spread1, spread2, keep0, keep1, right1, lead2, wide2, out_ref, pic):
     low = iota((32, 128), 1) < 64
     channel = (iota((256, 256), 0) // 84 == iota((256, 256), 1) // 64).astype(F32)
     for t in range(4):
@@ -657,12 +657,8 @@
             part = dot(x, spread0[:, j * 256 : j * 256 + 256]).astype(BF16) * keep0[...]
             fine.append(dot(lead0[...], part))
         total = jnp.concatenate([fine[j][h * 8 : h * 8 + 8] for h in range(2) for j in range(4)], axis=0)
-        mid = jnp.zeros((256, 256), F32)
-        for g in range(4):
-            some = slice(g * 256, g * 256 + 256)
-            mid = mid + dot(x, spread1[:, some]) * wide1[:, some].astype(F32)
-        mh, ml = split(mid)
-        total = total + dot(lead1[...], mh) + dot(lead1[...], ml)
+        mh, ml = split(dot(lead1[...], dot(x, spread1[...]).astype(BF16) * keep1[...]))
+        total = total + dot(mh, right1[...]) + dot(ml, right1[...])
         far = dot(x, spread2[...]) * wide2[...]
         far = far[:, :128] + far[:, 128:]
         far = far + pltpu.roll(far, 64, 1)

time: 76 us -> 76 us (level)
  no operation moved by 1% of the time
where the time goes in v7:
time: 76 us; the launch traced here: 75.9 us
  Pallas kernels  73 us (96%)
  local copies, waits for them, and re-layouts  1.62 us (2%)
  between operations  1.31 us (2%)
    pallas_call x1, Pallas kernels, blend(): pl.pallas_call(blend_kernel, out_shape=jax.ShapeDtypeStruct((3, 4, 4096),...  73 us
    unnamed x1, local copies, waits for them, and re-layouts  1.62 us

profile of v7, /device:TPU:1, one launch (start us, length us, event | category | flops | bytes accessed | tf_op | source)
XLA Modules:
  0.0 75.9 jit_solution(646283609565243436)
XLA Ops:
  1.3 73.0 %blend.1 = f32[3,4,4096]{2,1,0:T(4,128)} custom-call(s32[1]{0:T(128)S(6)} %copy.19.cell_ref, s32[1]{0:T(128)S(6)} %copy.20.partner_ref, s32[1,32]{1,0:T(1,128)} %bitcast.5, s32[1,32]{1,0:T(1,128)} %position_hbm.1, bf16[1,3,128,1024]{3,2,1,0:T(8,128)(2,1)} %frames_hbm.1, bf16[1,128,1024]{2,1,0:T(8,128)(2,1)} %weight_hbm.1, s32[1,64,128]{2,1,0:T(8,128)} %bitcast.4, ...), custom_call_target="tpu_custom_call" | custom-call | tf_op jit(solution)/shard_map/blend/pallas_call | solution.py:546
  74.3 1.6 %copy.21 = f32[4,3,4096]{2,0,1:T(4,128)} copy(f32[4,3,4096]{2,0,1:T(4,128)} %bitcast.3) | data formatting | bytes 393216
